TPU v7x, 128 devices: a whole 4x4x4 slice. The times are simulated.
128 devices in a mesh: space: 32 (over z, y_hi, x), sample: 4 (over y_lo, core).
Axes of the slice: x: 4, y: 4 (y_hi: 2, y_lo: 2; y = y_hi * 2 + y_lo), z: 4, core: 2. Of those that a mesh axis runs over, the one named last changes fastest.
Arguments:
- state_hat: float32 [20, 3, 256, 32, 128], P('sample', None, 'space'), may hold values from -2.4 to 2.4
- adjoint_hat: float32 [20, 3, 256, 32, 128], P('sample', None, 'space'), may hold values from -2.4 to 2.4
- objective_hat: float32 [20, 3, 256, 32, 128], P('sample', None, 'space'), may hold values from -6 to 6
- density: float32 [256, 32, 128], P('space'), may hold values from 0.05 to 1
- region: int32 [256, 32, 128], P('space'), may hold values from 0 to 3
Outputs:
- adjoint_residual: float32 [20, 3, 256, 32, 128], P('sample', None, 'space')
- density_gradient: float32 [256, 32, 128], P('space', 'sample')
All inputs are finite; a program needn't handle non-finite values.
Results may differ from a plain program's by a relative error of at most 0.00026.
Values sent between devices are 32-bit elements; how exact they have to be, the bound alone decides.
A program may use at most 128 MiB of HBM per device.

v0:
```python
import math

import jax
import jax.numpy as jnp
from jax import lax
from jax.sharding import PartitionSpec as P

NCOEF = 20
NT = 40


magnet_reluct = 0.95
iron_floor = 0.05
saturation = 1.0


def passed_along(array, axis, by):
    size = lax.axis_size(axis)
    pairs = [(i, i + by) for i in range(size) if 0 <= i + by < size]
    return lax.ppermute(array, axis, pairs)


def harmonic_table():
    sample_steps = jnp.arange(NT, dtype=jnp.int32).astype(jnp.float32)
    orders = (jnp.arange(NCOEF // 2, dtype=jnp.int32) + 1).astype(jnp.float32)
    angles = 2.0 * math.pi / NT * sample_steps[:, None] * orders[None, :]
    return jnp.stack([jnp.cos(angles), jnp.sin(angles)], axis=2).reshape(NT, NCOEF)


def forward_diff(potential, along):
    length = potential.shape[along]
    widths = [(0, 0)] * potential.ndim
    widths[along] = (0, 1)
    padded = jnp.pad(potential, widths)
    return lax.slice_in_dim(padded, 1, length + 1, axis=along) - potential


def backward_diff(potential, along):
    length = potential.shape[along]
    widths = [(0, 0)] * potential.ndim
    widths[along] = (1, 0)
    padded = jnp.pad(potential, widths)
    return lax.slice_in_dim(padded, 0, length, axis=along) - potential


def curl_field(potential, upper):
    x_step = jnp.concatenate([potential[:, :, 1:], upper], axis=2) - potential
    part_one, part_two, part_three = (potential[:, 0], potential[:, 1], potential[:, 2])
    flux_one = forward_diff(part_three, 2) - forward_diff(part_two, 3)
    flux_two = forward_diff(part_one, 3) - x_step[:, 2]
    flux_three = x_step[:, 1] - forward_diff(part_one, 2)
    return jnp.stack([flux_one, flux_two, flux_three], axis=1)


def curl_back(field_h, lower):
    x_step = jnp.concatenate([lower, field_h[:, 1:3, :-1]], axis=2) - field_h[:, 1:3]
    back_one = backward_diff(field_h[:, 1], 3) - backward_diff(field_h[:, 2], 2)
    back_two = x_step[:, 1] - backward_diff(field_h[:, 0], 3)
    back_three = backward_diff(field_h[:, 0], 2) - x_step[:, 0]
    return jnp.stack([back_one, back_two, back_three], axis=1)


def material(density, region):
    iron_share = jnp.where(region == 0, density**3, jnp.zeros_like(density))
    iron_slope = jnp.where(region == 0, 3.0 * density**2, jnp.zeros_like(density))
    base_reluct = jnp.where(
        region == 1, magnet_reluct * jnp.ones_like(density), jnp.ones_like(density)
    )
    return (iron_share, iron_slope, base_reluct)


def reluctivity(state_flux, adjoint_flux, base_reluct, iron_share):
    flux_square = jnp.sum(state_flux * state_flux, axis=1)
    flux_inner = jnp.sum(state_flux * adjoint_flux, axis=1)
    iron_curve = iron_floor + (1.0 - iron_floor) * flux_square / (flux_square + saturation)
    curve_slope = (1.0 - iron_floor) * saturation / (flux_square + saturation) ** 2
    reluct_now = base_reluct + iron_share * (iron_curve - 1.0)
    reluct_slope = iron_share * curve_slope
    field_h = (
        reluct_now[:, None] * adjoint_flux + (2.0 * reluct_slope * flux_inner)[:, None] * state_flux
    )
    return (field_h, iron_curve, flux_inner)


def local(state_hat, adjoint_hat, objective_hat, density, region):
    harm_table = harmonic_table()
    groups = lax.axis_size("sample")
    local_times = NT // groups
    planes = state_hat.shape[2]
    first_time = lax.axis_index("sample") * local_times
    own_rows = lax.dynamic_slice_in_dim(harm_table, first_time, local_times, 0)
    iron_share, iron_slope, base_reluct = material(density, region)
    columns = own_rows
    state_time = jnp.tensordot(
        columns,
        lax.all_gather(state_hat, "sample", axis=0, tiled=True),
        axes=1,
        precision=lax.Precision.HIGHEST,
    )
    adjoint_time = jnp.tensordot(
        columns,
        lax.all_gather(adjoint_hat, "sample", axis=0, tiled=True),
        axes=1,
        precision=lax.Precision.HIGHEST,
    )
    first_planes = jnp.concatenate([state_time[:, :, :1], adjoint_time[:, :, :1]], axis=1)
    upper = passed_along(first_planes, "space", -1)
    state_flux = curl_field(state_time, upper[:, :3])
    adjoint_flux = curl_field(adjoint_time, upper[:, 3:])
    field_h, iron_curve, flux_inner = reluctivity(state_flux, adjoint_flux, base_reluct, iron_share)
    lower = passed_along(field_h[:, 1:3, planes - 1 :], "space", 1)
    back_field = curl_back(field_h, lower)
    partial_terms = -(1.0 / NT) * jnp.sum(iron_slope * (iron_curve - 1.0) * flux_inner, axis=0)
    columns = own_rows
    summed = lax.psum_scatter(
        2.0 / NT * jnp.tensordot(columns.T, back_field, axes=1, precision=lax.Precision.HIGHEST),
        "sample",
        scatter_dimension=0,
        tiled=True,
    )
    density_gradient = lax.psum_scatter(partial_terms, "sample", scatter_dimension=1, tiled=True)
    adjoint_residual = objective_hat - summed
    return (adjoint_residual, density_gradient)


def solution(mesh):
    in_specs = (
        P("sample", None, "space", None, None),
        P("sample", None, "space", None, None),
        P("sample", None, "space", None, None),
        P("space", None, None),
        P("space", None, None),
    )
    out_specs = (P("sample", None, "space", None, None), P("space", "sample", None))
    return jax.shard_map(local, mesh=mesh, in_specs=in_specs, out_specs=out_specs, check_vma=False)
```

profile of v0, /device:TPU:1, one launch (start us, length us, event | category | flops | bytes accessed | tf_op | source)
XLA Modules:
  0.0 376.0 jit_solution(5956820325559077423)
XLA Ops:
  7.2 0.7 all-gather.3.cloned.1.call-update
  8.0 0.7 all-gather.5.cloned.1.call-update
  9.0 0.8 fusion.43
  9.8 80.5 %all-gather.3.cloned.1.call-done = f32[20,3,8,32,128]{4,3,2,1,0:T(8,128)} async-done(((f32[5,3,8,32,128]{4,3,2,1,0:T(8,128)}), f32[20,3,8,32,128]{4,3,2,1,0:T(8,128)}) %all-gather.3.cloned.1.call-update) | async-done | bytes 7864336 | tf_op jit(solution)/shard_map/all_gather | solution.py:96
  90.3 14.4 %fusion.2 = f32[10,3,8,32,128]{4,0,3,2,1:T(8,128)S(1)} fusion(f32[20,3,8,32,128]{4,3,2,1,0:T(8,128)} %all-gather.3.cloned.1.call-done, f32[40,20]{0,1:T(8,128)S(1)} %reshape.127, s32[]{:T(128)S(6)} %select_n.13), kind=kOutput, calls=%fused_computation.2 | convolution fusion | flops 235929600 | bytes 11799684 | tf_op jit(solution)/shard_map/dot_general | solution.py:94
  104.8 2.8 copy-done
  107.6 62.3 %all-gather.5.cloned.1.call-done = f32[20,3,8,32,128]{4,3,2,1,0:T(8,128)} async-done(((f32[5,3,8,32,128]{4,3,2,1,0:T(8,128)}), f32[20,3,8,32,128]{4,3,2,1,0:T(8,128)}) %all-gather.5.cloned.1.call-update) | async-done | bytes 7864336 | tf_op jit(solution)/shard_map/all_gather | solution.py:102
  169.9 14.4 %fusion = f32[10,3,8,32,128]{4,0,3,2,1:T(8,128)S(1)} fusion(f32[20,3,8,32,128]{4,3,2,1,0:T(8,128)} %all-gather.5.cloned.1.call-done, f32[40,20]{0,1:T(8,128)S(1)} %reshape.127, s32[]{:T(128)S(6)} %select_n.13), kind=kOutput, calls=%fused_computation | convolution fusion | flops 235929600 | bytes 11799684 | tf_op jit(solution)/shard_map/dot_general | solution.py:100
  184.9 1.3 collective-permute-start
  186.2 0.9 fusion.42
  187.0 2.2 slice-done
  189.2 0.7 slice-done.1
  189.9 2.8 slice_bitcast_fusion.13
  192.7 3.4 slice_bitcast_fusion.8
  196.1 13.5 %collective-permute-done = f32[10,6,1,32,128]{4,3,2,1,0:T(8,128)S(1)} collective-permute-done((f32[10,6,1,32,128]{4,3,2,1,0:T(8,128)S(1)}, f32[10,6,1,32,128]{4,3,2,1,0:T(8,128)S(1)}, u32[]{:S(2)}, u32[]{:S(2)}) %collective-permute-start) | collective-permute-done | bytes 983072 | tf_op jit(solution)/shard_map/ppermute | solution.py:20
  210.0 1.2 copy.26
  211.2 3.8 %maximum_subtract_fusion = f32[10,3,8,32,128]{4,0,3,2,1:T(8,128)} fusion(f32[10,3,8,32,128]{4,0,3,2,1:T(8,128)S(1)} %bitcast.77, f32[10,3,1,32,128]{4,0,3,2,1:T(8,128)S(1)} %copy.25, f32[10,3,7,32,128]{4,0,3,2,1:T(8,128)S(1)} %slice-done.4), kind=kLoop, calls=%fused_computation.4 | loop fusion | flops 1966080 | bytes 11796480 | tf_op jit(solution)/shard_map/sub | solution.py:47
  215.4 6.8 %maximum_subtract_fusion.1 = f32[10,3,8,32,128]{4,0,3,2,1:T(8,128)} fusion(f32[10,3,8,32,128]{4,0,3,2,1:T(8,128)} %copy-done.1, f32[10,3,1,32,128]{4,0,3,2,1:T(8,128)} %copy.26, f32[10,3,7,32,128]{4,0,3,2,1:T(8,128)S(1)} %slice-done.5), kind=kLoop, calls=%fused_computation.6 | loop fusion | flops 1966080 | bytes 11796480 | tf_op jit(solution)/shard_map/sub | solution.py:47
  222.3 5.8 %fusion.33 = (f32[10,1,8,32,128]{4,0,3,2,1:T(8,128)S(1)}, f32[10,1,8,32,128]{4,0,3,2,1:T(8,128)S(1)}, f32[10,1,8,32,128]{4,0,3,2,1:T(8,128)S(1)}) fusion(f32[10,8,32,128]{3,0,2,1:T(8,128)} %get-tuple-element.20, f32[10,3,8,32,128]{4,0,3,2,1:T(8,128)S(1)} %copy-done.2, f32[10,8,32,128]{3,0,2,1:T(8,128)S(1)} %copy-done.6, f32[10,8,32,128]{3,0,2,1:T(8,128)} %get-tuple-element.21), kind=kLoop, calls=%fused_computation.52 | loop fusion | flops 2293760 | bytes 10485760 | tf_op jit(solution)/shard_map/stack | solution.py:52
  230.0 1.7 fusion.37
  231.7 2.0 multiply_reduce_fusion.1
  233.8 1.6 multiply_reduce_fusion.2
  235.4 1.1 multiply_add_fusion
  237.4 3.1 collective-permute-start.1
  241.2 10.5 %collective-permute-done.1 = f32[10,2,1,32,128]{4,0,3,2,1:T(8,128)S(1)} collective-permute-done((f32[10,2,1,32,128]{4,0,3,2,1:T(8,128)S(1)}, f32[10,2,1,32,128]{4,0,3,2,1:T(8,128)S(1)}, u32[]{:S(2)}, u32[]{:S(2)}) %collective-permute-start.1) | collective-permute-done | bytes 327712 | tf_op jit(solution)/shard_map/ppermute | solution.py:20
  252.3 0.7 fusion.41
  253.1 8.6 %broadcast_multiply_fusion = f32[20,3,8,32,128]{4,0,3,2,1:T(8,128)S(1)} fusion(f32[10,1,8,32,128]{4,0,3,2,1:T(8,128)S(1)} %get-tuple-element.18, f32[10,1,8,32,128]{4,0,3,2,1:T(8,128)S(1)} %get-tuple-element.17, f32[10,1,8,32,128]{4,0,3,2,1:T(8,128)S(1)} %fusion.26, f32[40,20]{0,1:T(8,128)S(1)} %reshape.127, s32[]{:T(128)S(6)} %select_n.13), kind=kOutput, calls=%fused_computation.17 | convolution fusion | flops 239861760 | bytes 11799684 | tf_op jit(solution)/shard_map/dot_general | solution.py:116
  261.7 4.5 %copy.22 = f32[20,3,8,32,128]{4,3,2,1,0:T(8,128)} copy(f32[20,3,8,32,128]{4,0,3,2,1:T(8,128)S(1)} %broadcast_multiply_fusion) | data formatting | bytes 15728640 | tf_op jit(solution)/shard_map/mul | solution.py:116
  266.3 0.7 broadcast_multiply_fusion.1
  267.0 81.5 %reduce-scatter.3.cloned.1.call-done = f32[5,3,8,32,128]{4,3,2,1,0:T(8,128)} async-done(((f32[20,3,8,32,128]{4,3,2,1,0:T(8,128)}), f32[5,3,8,32,128]{4,3,2,1,0:T(8,128)}) %reduce-scatter.3.cloned.1.call-update) | async-done | bytes 1966096 | tf_op jit(solution)/shard_map/reduce_scatter | solution.py:115
  348.4 3.3 sub.107
  351.7 17.7 %reduce-scatter.5.cloned.1.call-done = f32[8,8,128]{2,1,0:T(8,128)} async-done(((f32[8,32,128]{2,1,0:T(8,128)}), f32[8,8,128]{2,1,0:T(8,128)}) %reduce-scatter.5.cloned.1.call-update) | async-done | bytes 32784 | tf_op jit(solution)/shard_map/reduce_scatter | solution.py:121
  (64 shorter events, 5.7 us)
Async XLA Ops:
  7.2 1.8 copy-start.11
  7.2 1.8 copy-start.12
  7.2 83.1 %all-gather.3.cloned.1.call-start = ((), (), s32[]{:S(2)}) async-start(), calls=%async_computation.2 | async-start | bytes 9830400 | tf_op jit(solution)/shard_map/all_gather | solution.py:96
  7.9 162.0 %all-gather.5.cloned.1.call-start = ((), (), s32[]{:S(2)}) async-start(), calls=%async_computation.3 | async-start | bytes 9830400 | tf_op jit(solution)/shard_map/all_gather | solution.py:102
  8.7 339.8 %reduce-scatter.3.cloned.1.call-start = ((), (), s32[]{:S(2)}) async-start(), calls=%async_computation.4 | async-start | bytes 9830400 | tf_op jit(solution)/shard_map/reduce_scatter | solution.py:115
  104.8 2.8 copy-start
  184.3 8.4 %copy-start.1 = (f32[10,3,8,32,128]{4,0,3,2,1:T(8,128)}, f32[10,3,8,32,128]{4,0,3,2,1:T(8,128)S(1)}, u32[]{:S(2)}) copy-start(f32[10,3,8,32,128]{4,0,3,2,1:T(8,128)S(1)} %fusion) | copy-start | bytes 11796484
  184.9 24.8 %collective-permute-start = (f32[10,6,1,32,128]{4,3,2,1,0:T(8,128)S(1)}, f32[10,6,1,32,128]{4,3,2,1,0:T(8,128)S(1)}, u32[]{:S(2)}, u32[]{:S(2)}) collective-permute-start(f32[10,6,1,32,128]{4,3,2,1,0:T(8,128)S(1)} %copy.19), channel_id=1, source_target_pairs={{4,0},{8,4},{12,8},{16,12},{20,16},{24,20},{28,24},{32,28},{36,32}... | collective-permute-start | bytes 2949128 | tf_op jit(solution)/shard_map/ppermute | solution.py:20
  187.0 2.2 slice-start
  187.0 2.9 slice-start.1
  189.9 21.3 %slice-start.2 = ((s8[6291456]{0:T(1024)(128)(4,1)}), s8[2097152]{0:T(1024)(128)(4,1)S(1)}, s32[]{:S(2)}) async-start(s8[6291456]{0:T(1024)(128)(4,1)} %bitcast.76), calls=%async_computation.8 | async-start | bytes 4194304
  192.7 18.5 %slice-start.3 = ((s8[6291456]{0:T(1024)(128)(4,1)}), s8[4194304]{0:T(1024)(128)(4,1)S(1)}, s32[]{:S(2)}) async-start(s8[6291456]{0:T(1024)(128)(4,1)} %bitcast.76), calls=%async_computation.9 | async-start | bytes 8388608
  192.7 18.5 %slice-start.4 = ((f32[10,3,8,32,128]{4,0,3,2,1:T(8,128)}), f32[10,3,7,32,128]{4,0,3,2,1:T(8,128)S(1)}, s32[]{:S(2)}) async-start(f32[10,3,8,32,128]{4,0,3,2,1:T(8,128)} %copy-done), calls=%async_computation.10 | async-start | bytes 11010048 | tf_op jit(solution)/shard_map/slice | solution.py:47
  211.2 4.2 %slice-start.5 = ((f32[10,3,8,32,128]{4,0,3,2,1:T(8,128)}), f32[10,3,7,32,128]{4,0,3,2,1:T(8,128)S(1)}, s32[]{:S(2)}) async-start(f32[10,3,8,32,128]{4,0,3,2,1:T(8,128)} %copy-done.1), calls=%async_computation.11 | async-start | bytes 11010048 | tf_op jit(solution)/shard_map/slice | solution.py:47
  215.4 6.8 %copy-start.2 = (f32[10,3,8,32,128]{4,0,3,2,1:T(8,128)S(1)}, f32[10,3,8,32,128]{4,0,3,2,1:T(8,128)}, u32[]{:S(2)}) copy-start(f32[10,3,8,32,128]{4,0,3,2,1:T(8,128)} %maximum_subtract_fusion) | copy-start | bytes 11796484
  215.4 6.8 %copy-start.6 = (f32[10,8,32,128]{3,0,2,1:T(8,128)S(1)}, f32[10,8,32,128]{3,0,2,1:T(8,128)}, u32[]{:S(2)}) copy-start(f32[10,8,32,128]{3,0,2,1:T(8,128)} %get-tuple-element.19) | copy-start | bytes 3932164
  222.3 5.9 %slice-start.6 = ((s8[6291456]{0:T(1024)(128)(4,1)}), s8[4194304]{0:T(1024)(128)(4,1)S(1)}, s32[]{:S(2)}) async-start(s8[6291456]{0:T(1024)(128)(4,1)} %bitcast.78), calls=%async_computation.12 | async-start | bytes 8388608
  222.3 5.9 %slice-start.7 = ((s8[6291456]{0:T(1024)(128)(4,1)}), s8[2097152]{0:T(1024)(128)(4,1)S(1)}, s32[]{:S(2)}) async-start(s8[6291456]{0:T(1024)(128)(4,1)} %bitcast.78), calls=%async_computation.13 | async-start | bytes 4194304
  222.3 6.5 %copy-start.3 = (f32[10,8,32,128]{3,0,2,1:T(8,128)S(1)}, f32[10,8,32,128]{3,0,2,1:T(8,128)}, u32[]{:S(2)}) copy-start(f32[10,8,32,128]{3,0,2,1:T(8,128)} %get-tuple-element.22) | copy-start | bytes 3932164
  222.3 7.1 %copy-start.4 = (f32[10,8,32,128]{3,0,2,1:T(8,128)S(1)}, f32[10,8,32,128]{3,0,2,1:T(8,128)}, u32[]{:S(2)}) copy-start(f32[10,8,32,128]{3,0,2,1:T(8,128)} %get-tuple-element.23) | copy-start | bytes 3932164
  222.3 7.7 %copy-start.5 = (f32[10,8,32,128]{3,0,2,1:T(8,128)S(1)}, f32[10,8,32,128]{3,0,2,1:T(8,128)}, u32[]{:S(2)}) copy-start(f32[10,8,32,128]{3,0,2,1:T(8,128)} %get-tuple-element.24) | copy-start | bytes 3932164
  231.7 2.1 copy-start.8
  231.7 2.1 copy-start.9
  231.7 2.1 copy-start.10
  237.4 14.3 %collective-permute-start.1 = (f32[10,2,1,32,128]{4,0,3,2,1:T(8,128)S(1)}, f32[10,2,1,32,128]{4,0,3,2,1:T(8,128)S(1)}, u32[]{:S(2)}, u32[]{:S(2)}) collective-permute-start(f32[10,2,1,32,128]{4,0,3,2,1:T(8,128)S(1)} %slice.163), channel_id=1, source_target_pairs={{0,4},{4,8},{8,12},{12,16},{16,20},{20,24},{24,28},{28,32},{32,36}... | collective-permute-start | bytes 983048 | tf_op jit(solution)/shard_map/ppermute | solution.py:20
  266.2 82.2 %copy-start.7 = (f32[5,3,8,32,128]{4,3,2,1,0:T(8,128)S(1)}, f32[5,3,8,32,128]{4,3,2,1,0:T(8,128)}, u32[]{:S(2)}) copy-start(f32[5,3,8,32,128]{4,3,2,1,0:T(8,128)} %param.7) | copy-start | bytes 5898244
  266.2 103.2 %reduce-scatter.5.cloned.1.call-start = ((), (), s32[]{:S(2)}) async-start(), calls=%async_computation.5 | async-start | bytes 163840 | tf_op jit(solution)/shard_map/reduce_scatter | solution.py:121
Sparse Core Ops, SparseCore 0:
  9.7 80.6 all-gather.2
  92.0 77.8 all-gather.4
  266.4 82.0 reduce-scatter.2
  351.2 18.1 reduce-scatter.4
where the time goes:
time: 376 us
  waiting for transfers between devices  268 us (71%)
  matrix products  37.5 us (10%)
  other arithmetic  30.8 us (8%)
  local copies, waits for them, and re-layouts  21.4 us (6%)
  between operations  14.1 us (4%)
  starting transfers between devices  4.57 us (1%)
    reduce_scatter x1, waiting for transfers between devices, local(): lax.psum_scatter(2.0 / NT * jnp.tensordot(columns.T, back_field, axes=1,...  81.5 us
    all_gather x1, waiting for transfers between devices, local(): lax.all_gather(state_hat, 'sample', axis=0, tiled=True)  80.5 us
    all_gather x1, waiting for transfers between devices, local(): lax.all_gather(adjoint_hat, 'sample', axis=0, tiled=True)  62.3 us
    ppermute x2, waiting for transfers between devices, passed_along(): return lax.ppermute(array, axis, pairs)  24.1 us
    reduce_scatter x1, waiting for transfers between devices, local(): lax.psum_scatter(partial_terms, 'sample', scatter_dimension=1, tiled=True)  17.7 us
    dot_general x1, matrix products, local(): jnp.tensordot(columns, lax.all_gather(state_hat, 'sample', axis=0, tiled=...  14.4 us
    dot_general x1, matrix products, local(): jnp.tensordot(columns, lax.all_gather(adjoint_hat, 'sample', axis=0, tile...  14.4 us
    sub x2, other arithmetic, curl_field(): x_step = jnp.concatenate([potential[:, :, 1:], upper], axis=2) - potential  10.7 us
  transfers between devices with their start and end apart: 6, of which 6 were waited for; matrix products, arithmetic and copies ran while one was open for 7% of the time, Pallas kernels for 0%

commit v1 on v0

v1 whole, which is shorter than its diff:
```python
import functools
import math

import jax
import jax.numpy as jnp
from jax import lax
from jax.experimental import pallas as pl
from jax.experimental.pallas import tpu as pltpu
from jax.sharding import PartitionSpec as P

NT = 40
NCOEF = 20
NY = 32
NZ = 128
PLANES = 8
GROUP = 4
OWN = NCOEF // GROUP
ROWS = NY // GROUP
FOLDS = NT // 4 + 1

magnet_reluct = 0.95
iron_floor = 0.05

CLASSES = (
    ("cos", (2, 4, 6, 8, 10)),
    ("cos", (1, 3, 5, 7, 9)),
    ("sin", (2, 4, 6, 8, 10)),
    ("sin", (1, 3, 5, 7, 9)),
)


def coef_index(kind, order):
    return 2 * (order - 1) + (0 if kind == "cos" else 1)


def factor(kind, order, n):
    turn = (n * order) % NT
    quarter = NT // 4
    if kind == "sin":
        turn = (turn - quarter) % NT
    if turn % quarter == 0:
        return (1.0, 0.0, -1.0, 0.0)[turn // quarter]
    if turn * 3 % NT == 0 and False:
        return 0.0
    return math.cos(2.0 * math.pi * turn / NT)


def combine(terms, constants):
    total = None
    for term, constant in zip(terms, constants):
        if constant == 0.0:
            continue
        if constant == 1.0:
            piece = term
        elif constant == -1.0:
            piece = -term
        else:
            piece = term * jnp.float32(constant)
        total = piece if total is None else total + piece
    return jnp.zeros_like(terms[0]) if total is None else total


def plane_at(k):
    return lax.rem(k + PLANES // 2, PLANES)


def kernel(
    state_hbm, adjoint_hbm, objective_hbm, density_hbm, region_hbm,
    out_hbm, grad_hbm,
    pot, obj, dens, regn, upper, lower, send, recv, hsend, hrecv, wave, fold, out, grad,
    in_sems, obj_sem, mat_sems, up_send, up_recv, low_send, low_recv,
    f_send, f_recv, b_send, b_recv, out_sems, grad_sem,
):
    me = lax.axis_index("sample")
    block = lax.axis_index("space")
    blocks = lax.axis_size("space")
    above = lax.rem(block + 1, blocks)
    below = lax.rem(block + blocks - 1, blocks)

    def load(k):
        p = plane_at(k)
        return [
            pltpu.make_async_copy(ref.at[:, :, p], pot.at[i, p], in_sems.at[i, p])
            for i, ref in enumerate((state_hbm, adjoint_hbm))
        ]

    @pl.loop(0, PLANES)
    def _(k):
        for copy in load(k):
            copy.start()

    rows = pl.ds(pl.multiple_of(me * ROWS, ROWS), ROWS)
    material = [
        pltpu.make_async_copy(density_hbm.at[:, rows], dens, mat_sems.at[0]),
        pltpu.make_async_copy(region_hbm.at[:, rows], regn, mat_sems.at[1]),
    ]
    for copy in material:
        copy.start()
    objective = pltpu.make_async_copy(objective_hbm, obj, obj_sem)
    objective.start()

    peers = [lax.rem(me + r, GROUP) for r in range(1, GROUP)]
    barrier = pltpu.get_barrier_semaphore()
    for peer in peers:
        pl.semaphore_signal(barrier, inc=1, device_id={"sample": peer}, device_id_type=pl.DeviceIdType.MESH)
    for other in (above, below):
        pl.semaphore_signal(barrier, inc=1, device_id={"space": other}, device_id_type=pl.DeviceIdType.MESH)
    pl.semaphore_wait(barrier, GROUP + 1)

    ups = [
        pltpu.make_async_remote_copy(
            src_ref=ref.at[:, 1:3, 0], dst_ref=upper.at[i],
            send_sem=up_send.at[i], recv_sem=up_recv.at[i],
            device_id={"space": below}, device_id_type=pl.DeviceIdType.MESH,
        )
        for i, ref in enumerate((state_hbm, adjoint_hbm))
    ]
    for copy in ups:
        copy.start()

    def forward(p):
        return [
            pltpu.make_async_remote_copy(
                src_ref=send.at[p, peer], dst_ref=recv.at[p, me],
                send_sem=f_send.at[p, r], recv_sem=f_recv.at[p, r],
                device_id={"sample": peer}, device_id_type=pl.DeviceIdType.MESH,
            )
            for r, peer in enumerate(peers)
        ]

    def backward(p):
        return [
            pltpu.make_async_remote_copy(
                src_ref=hsend.at[p, peer], dst_ref=hrecv.at[p, me],
                send_sem=b_send.at[p, r], recv_sem=b_recv.at[p, r],
                device_id={"sample": peer}, device_id_type=pl.DeviceIdType.MESH,
            )
            for r, peer in enumerate(peers)
        ]

    row_id = lax.broadcasted_iota(jnp.int32, (NY, NZ), 0)
    lane_id = lax.broadcasted_iota(jnp.int32, (NY, NZ), 1)

    def next_row(a):
        return jnp.where(row_id == NY - 1, 0.0, pltpu.roll(a, NY - 1, 0))

    def next_lane(a):
        return jnp.where(lane_id == NZ - 1, 0.0, pltpu.roll(a, NZ - 1, 1))

    def prior_row(a):
        return jnp.where(row_id == 0, 0.0, pltpu.roll(a, 1, 0))

    def prior_lane(a):
        return jnp.where(lane_id == 0, 0.0, pltpu.roll(a, 1, 1))

    def curl(p, j, i, up_one, up_two):
        zero, one, two = pot[i, p, j, 0], pot[i, p, j, 1], pot[i, p, j, 2]
        first = (next_row(two) - two) - (next_lane(one) - one)
        second = (next_lane(zero) - zero) - (up_two - two)
        third = (up_one - one) - (next_row(zero) - zero)
        for c, part in enumerate((first, second, third)):
            send[p, :, 3 * i + c, j] = part.reshape(GROUP, ROWS, NZ)

    def finish_curl(p):
        recv[p, me] = send[p, me]
        for copy in forward(p)[1:] + forward(p)[:1]:
            copy.start()

    @pl.loop(0, PLANES)
    def _(k):
        p = plane_at(k)

        @pl.when(k == 0)
        def _():
            for copy in load(k):
                copy.wait()

        @pl.when((k < PLANES - 1) & (k != PLANES // 2 - 1))
        def _():
            for copy in load(k + 1):
                copy.wait()

        @pl.when(p < PLANES - 1)
        def _():
            @pl.loop(0, OWN)
            def _(j):
                for i in range(2):
                    curl(p, j, i, pot[i, p + 1, j, 1], pot[i, p + 1, j, 2])

        @pl.when(p == PLANES - 1)
        def _():
            for copy in load(k + 1):
                copy.wait()
            for copy in ups:
                copy.wait_recv()
            last = block == blocks - 1

            @pl.loop(0, OWN)
            def _(j):
                for i in range(2):
                    curl(
                        PLANES - 1, j, i,
                        jnp.where(last, 0.0, upper[i, j, 0]),
                        jnp.where(last, 0.0, upper[i, j, 1]),
                    )

        finish_curl(p)

    for copy in material:
        copy.wait()

    def nonlinear(p):
        @pl.loop(0, 6)
        def _(pc):
            for t, (kind, orders) in enumerate(CLASSES):
                where = [coef_index(kind, m) for m in orders]
                terms = [recv[p, c // OWN, pc, c % OWN] for c in where]
                for n in range(FOLDS):
                    wave[n, t, pc] = combine(terms, [factor(kind, m, n) for m in orders])

        density, region = dens[p], regn[p]
        iron = region == 0
        share = jnp.where(iron, density * density * density, 0.0) * jnp.float32(1.0 - iron_floor)
        slope = jnp.where(iron, 3.0 * density * density, 0.0)
        base = jnp.where(region == 1, jnp.float32(magnet_reluct), jnp.float32(1.0))

        def samples(n, total):
            state = [[], [], []]
            adjoint = [[], [], []]
            for pc in range(6):
                ce, co, se, so = (wave[n, t, pc] for t in range(4))
                a, b, d, f = ce + co, ce - co, se + so, se - so
                (state if pc < 3 else adjoint)[pc % 3] = (a + d, a - d, b - f, b + f)
            field = [[], [], []]
            part = None
            for v in range(4):
                s = [state[c][v] for c in range(3)]
                g = [adjoint[c][v] for c in range(3)]
                square = s[0] * s[0] + s[1] * s[1] + s[2] * s[2]
                inner = s[0] * g[0] + s[1] * g[1] + s[2] * g[2]
                r = 1.0 / (square + 1.0)
                t = share * r
                ri = r * inner
                nu = base - t
                mu = (t + t) * ri
                part = ri if part is None else part + ri
                for c in range(3):
                    field[c].append(nu * g[c] + mu * s[c])
            for c in range(3):
                w, x, y, z = field[c]
                a, d = w + x, w - x
                b, f = z + y, z - y
                fold[n, 0, c] = a + b
                fold[n, 1, c] = a - b
                fold[n, 2, c] = d + f
                fold[n, 3, c] = d - f
            ends = (n == 0) | (n == FOLDS - 1)
            return total + part * jnp.where(ends, 0.5, 1.0)

        total = lax.fori_loop(0, FOLDS, samples, jnp.zeros((ROWS, NZ), jnp.float32))
        grad[p] = total * slope * jnp.float32((1.0 - iron_floor) / NT)

        @pl.loop(0, 3)
        def _(c):
            for t, (kind, orders) in enumerate(CLASSES):
                terms = [fold[n, t, c] for n in range(FOLDS)]
                terms[0] = terms[0] * 0.5
                terms[-1] = terms[-1] * 0.5
                for m in orders:
                    got = combine(terms, [factor(kind, m, n) for n in range(FOLDS)])
                    at = coef_index(kind, m)
                    hsend[p, at // OWN, at % OWN, c] = got * jnp.float32(2.0 / NT)

    @pl.loop(0, PLANES)
    def _(k):
        p = plane_at(k)
        for copy in forward(p):
            copy.wait_recv()
        nonlinear(p)
        hrecv[p, me] = hsend[p, me]
        for copy in backward(p)[1:] + backward(p)[:1]:
            copy.start()

    gradient = pltpu.make_async_copy(grad, grad_hbm, grad_sem)
    gradient.start()

    down = pltpu.make_async_remote_copy(
        src_ref=hrecv.at[PLANES - 1, :, :, 1:3], dst_ref=lower,
        send_sem=low_send, recv_sem=low_recv,
        device_id={"space": above}, device_id_type=pl.DeviceIdType.MESH,
    )

    def whole(ref, p, j, c):
        return ref[p, :, j, c].reshape(NY, NZ)

    def store(p):
        return pltpu.make_async_copy(out.at[p], out_hbm.at[:, :, p], out_sems.at[p])

    def curl_back(p, j, low_one, low_two):
        zero, one, two = (whole(hrecv, p, j, c) for c in range(3))
        x_one, x_two = low_one - one, low_two - two
        first = (prior_lane(one) - one) - (prior_row(two) - two)
        second = x_two - (prior_lane(zero) - zero)
        third = (prior_row(zero) - zero) - x_one
        for c, part in enumerate((first, second, third)):
            out[p, j, c] = obj[j, c, p] - part

    def inner_plane(p):
        @pl.loop(0, OWN)
        def _(j):
            curl_back(p, j, whole(hrecv, p - 1, j, 1), whole(hrecv, p - 1, j, 2))

        store(p).start()

    objective.wait()

    @pl.loop(0, PLANES)
    def _(k):
        p = plane_at(k)
        for copy in backward(p):
            copy.wait_recv()

        @pl.when(p == PLANES - 1)
        def _():
            down.start()

        @pl.when((k > 0) & (p > 0))
        def _():
            inner_plane(p)

        @pl.when(p == 0)
        def _():
            down.wait_recv()
            first = block == 0

            @pl.loop(0, OWN)
            def _(j):
                curl_back(
                    0, j,
                    jnp.where(first, 0.0, lower[:, j, 0].reshape(NY, NZ)),
                    jnp.where(first, 0.0, lower[:, j, 1].reshape(NY, NZ)),
                )

            store(p).start()

    inner_plane(PLANES // 2)

    gradient.wait()
    for copy in ups:
        copy.wait_send()
    down.wait_send()

    @pl.loop(0, PLANES)
    def _(p):
        store(p).wait()
        for copy in forward(p) + backward(p):
            copy.wait_send()


def local(state_hat, adjoint_hat, objective_hat, density, region):
    f32 = jnp.float32
    hbm = pl.BlockSpec(memory_space=pl.ANY)
    dma = pltpu.SemaphoreType.DMA
    return pl.pallas_call(
        kernel,
        out_shape=(
            jax.ShapeDtypeStruct((OWN, 3, PLANES, NY, NZ), f32),
            jax.ShapeDtypeStruct((PLANES, ROWS, NZ), f32),
        ),
        in_specs=[hbm] * 5,
        out_specs=(hbm, hbm),
        scratch_shapes=[
            pltpu.VMEM((2, PLANES, OWN, 3, NY, NZ), f32),
            pltpu.VMEM((OWN, 3, PLANES, NY, NZ), f32),
            pltpu.VMEM((PLANES, ROWS, NZ), f32),
            pltpu.VMEM((PLANES, ROWS, NZ), jnp.int32),
            pltpu.VMEM((2, OWN, 2, NY, NZ), f32),
            pltpu.VMEM((GROUP, OWN, 2, ROWS, NZ), f32),
            pltpu.VMEM((PLANES, GROUP, 6, OWN, ROWS, NZ), f32),
            pltpu.VMEM((PLANES, GROUP, 6, OWN, ROWS, NZ), f32),
            pltpu.VMEM((PLANES, GROUP, OWN, 3, ROWS, NZ), f32),
            pltpu.VMEM((PLANES, GROUP, OWN, 3, ROWS, NZ), f32),
            pltpu.VMEM((FOLDS, 4, 6, ROWS, NZ), f32),
            pltpu.VMEM((FOLDS, 4, 3, ROWS, NZ), f32),
            pltpu.VMEM((PLANES, OWN, 3, NY, NZ), f32),
            pltpu.VMEM((PLANES, ROWS, NZ), f32),
            dma((2, PLANES)), dma, dma((2,)), dma((2,)), dma((2,)), dma, dma,
            dma((PLANES, GROUP - 1)), dma((PLANES, GROUP - 1)),
            dma((PLANES, GROUP - 1)), dma((PLANES, GROUP - 1)),
            dma((PLANES,)), dma,
        ],
        compiler_params=pltpu.CompilerParams(
            collective_id=0, has_side_effects=True, vmem_limit_bytes=60 * 1024 * 1024
        ),
    )(state_hat, adjoint_hat, objective_hat, density, region)


def solution(mesh):
    in_specs = (
        P("sample", None, "space", None, None),
        P("sample", None, "space", None, None),
        P("sample", None, "space", None, None),
        P("space", None, None),
        P("space", None, None),
    )
    out_specs = (P("sample", None, "space", None, None), P("space", "sample", None))
    return jax.shard_map(local, mesh=mesh, in_specs=in_specs, out_specs=out_specs, check_vma=False)
```

time: 376 us -> 86.2 us (0.23)
  waiting for transfers between devices: 268 us -> 0 us
  Pallas kernels: 0 us -> 81.7 us
  matrix products: 37.5 us -> 0 us
  other arithmetic: 30.8 us -> 0 us
  local copies, waits for them, and re-layouts: 21.4 us -> 3.66 us
  between operations: 14.1 us -> 0.65 us
  starting transfers between devices: 4.57 us -> 0 us
    all_gather x2 -> x0, waiting for transfers between devices: 143 us -> none  [the longest x1 80.5 us: local(): lax.all_gather(state_hat, 'sample', axis=0, tiled=True)]
    reduce_scatter x2 -> x0, waiting for transfers between devices: 99.2 us -> none  [the longest x1 81.5 us: local(): lax.psum_scatter(2.0 / NT * jnp.tensordot(columns.T, back_field, axes=1,...]
    pallas_call x0 -> x1, Pallas kernels: none -> 81.7 us  [local(): pl.pallas_call(kernel, out_shape=(jax.ShapeDtypeStruct((OWN, 3, PLANES, N...]
    dot_general x3 -> x0, matrix products: 37.5 us -> none  [the longest x1 14.4 us: local(): jnp.tensordot(columns, lax.all_gather(state_hat, 'sample', axis=0, tiled=...]
    ppermute x2 -> x0, waiting for transfers between devices: 24.1 us -> none  [passed_along(): return lax.ppermute(array, axis, pairs)]
    sub x4 -> x0, other arithmetic: 14.5 us -> none  [the longest x2 10.7 us: curl_field(): x_step = jnp.concatenate([potential[:, :, 1:], upper], axis=2) - potential]
    another operation x5 -> x0, other arithmetic: 8.92 us -> none  [the longest x2 7.55 us: curl_field(): return jnp.stack([flux_one, flux_two, flux_three], axis=1)]
    squeeze x3 -> x0, local copies, waits for them, and re-layouts: 6.77 us -> none  [the longest x2 6.17 us: curl_field(): potential[:, 1]]
  transfers between devices with their start and end apart: 6 -> 0, of which waited for: 6 -> 0; matrix products, arithmetic and copies ran while one was open for 7% -> 0% of each run, Pallas kernels for 0% -> 0%
where the time goes in v1:
time: 86.2 us; the launch traced here: 86 us
  Pallas kernels  81.7 us (95%)
  local copies, waits for them, and re-layouts  3.66 us (4%)
    pallas_call x1, Pallas kernels, local(): pl.pallas_call(kernel, out_shape=(jax.ShapeDtypeStruct((OWN, 3, PLANES, N...  81.7 us
    unnamed x4, local copies, waits for them, and re-layouts  3.66 us

profile of v1, /device:TPU:1, one launch (start us, length us, event | category | flops | bytes accessed | tf_op | source)
XLA Modules:
  0.0 86.0 jit_solution(3287795126167408817)
XLA Ops:
  0.6 81.7 %shard_map.68 = (f32[5,3,8,32,128]{4,3,2,1,0:T(8,128)}, f32[8,8,128]{2,1,0:T(8,128)}) custom-call(f32[5,3,8,32,128]{4,3,2,1,0:T(8,128)} %state_hbm.1, f32[5,3,8,32,128]{4,3,2,1,0:T(8,128)} %adjoint_hbm.1, f32[5,3,8,32,128]{4,3,2,1,0:T(8,128)} %objective_hbm.1, f32[8,32,128]{2,1,0:T(8,128)} %density_hbm.1, s32[8,32,128]{2,1,0:T(8,128)} %region_hbm.1), custom_call_target="tpu_custom_call" | custom-call | tf_op jit(solution)/shard_map/pallas_call | solution.py:364
  82.4 0.0 copy-start
  82.4 3.0 %copy.9 = f32[5,3,8,32,128]{4,3,2,1,0:T(8,128)} copy(f32[5,3,8,32,128]{4,3,2,1,0:T(8,128)} %get-tuple-element.4) | data formatting | bytes 3932160
  85.4 0.0 copy-done
  85.4 0.6 copy.10
Async XLA Ops:
  82.4 3.1 %copy-start = (f32[8,8,128]{2,1,0:T(8,128)S(1)}, f32[8,8,128]{2,1,0:T(8,128)}, u32[]{:S(2)}) copy-start(f32[8,8,128]{2,1,0:T(8,128)} %get-tuple-element.5) | copy-start | bytes 98308

commit v2 on v1

v2 whole, which is shorter than its diff:
```python
import math

import jax
import jax.numpy as jnp
from jax import lax
from jax.experimental import pallas as pl
from jax.experimental.pallas import tpu as pltpu
from jax.sharding import PartitionSpec as P

NT = 40
NCOEF = 20
NY = 32
NZ = 128
PLANES = 8
GROUP = 4
OWN = NCOEF // GROUP
ROWS = NY // GROUP
FOLDS = NT // 4 + 1
PAIRS = 2 * OWN
RUN = 4

magnet_reluct = 0.95
iron_floor = 0.05

CLASSES = (
    ("cos", (2, 4, 6, 8, 10)),
    ("cos", (1, 3, 5, 7, 9)),
    ("sin", (2, 4, 6, 8, 10)),
    ("sin", (1, 3, 5, 7, 9)),
)


def coef_index(kind, order):
    return 2 * (order - 1) + (0 if kind == "cos" else 1)


def factor(kind, order, n):
    turn = (n * order) % NT
    quarter = NT // 4
    if kind == "sin":
        turn = (turn - quarter) % NT
    if turn % quarter == 0:
        return (1.0, 0.0, -1.0, 0.0)[turn // quarter]
    return math.cos(2.0 * math.pi * turn / NT)


def combine(terms, constants):
    total = None
    for term, constant in zip(terms, constants):
        if constant == 0.0:
            continue
        if constant == 1.0:
            piece = term
        elif constant == -1.0:
            piece = -term
        else:
            piece = term * jnp.float32(constant)
        total = piece if total is None else total + piece
    return jnp.zeros_like(terms[0]) if total is None else total


def kernel(
    state_hbm, adjoint_hbm, objective_hbm, density_hbm, region_hbm,
    out_hbm, grad_hbm,
    pot, phi, obj, dens, regn, upper, lower, send, recv, phi_send, phi_recv,
    hsend, hrecv, flux, wave, fold, psi, out, grad, grad_in,
    in_sems, obj_sem, mat_sems, up_send, up_recv, low_send, low_recv,
    f_send, f_recv, b_send, b_recv, g_send, g_recv, out_sems, grad_sem,
):
    me = lax.axis_index("sample")
    block = lax.axis_index("space")
    blocks = lax.axis_size("space")
    above = lax.rem(block + 1, blocks)
    below = lax.rem(block + blocks - 1, blocks)
    mesh_id = pl.DeviceIdType.MESH

    def turned(index, where):
        return lax.rem(index + 2 * lax.rem(where // RUN, 2), GROUP)

    odd = lax.rem(block // RUN, 2)
    slab = turned(me, block)
    up_id = {"space": above, "sample": turned(slab, above)}
    down_id = {"space": below, "sample": turned(slab, below)}
    peers = [lax.rem(me + r, GROUP) for r in (2, 3, 1)]

    def load(p):
        return [
            pltpu.make_async_copy(ref.at[:, :, p], pot.at[i, p], in_sems.at[i, p])
            for i, ref in enumerate((state_hbm, adjoint_hbm))
        ]

    @pl.loop(0, PLANES)
    def _(p):
        for copy in load(p):
            copy.start()

    rows = pl.ds(pl.multiple_of(slab * ROWS, ROWS), ROWS)
    material = [
        pltpu.make_async_copy(density_hbm.at[:, rows], dens, mat_sems.at[0]),
        pltpu.make_async_copy(region_hbm.at[:, rows], regn, mat_sems.at[1]),
    ]
    for copy in material:
        copy.start()
    objective = pltpu.make_async_copy(objective_hbm, obj, obj_sem)
    objective.start()

    barrier = pltpu.get_barrier_semaphore()
    for peer in peers:
        pl.semaphore_signal(barrier, inc=1, device_id={"sample": peer}, device_id_type=mesh_id)
    for other in (up_id, down_id):
        pl.semaphore_signal(barrier, inc=1, device_id=other, device_id_type=mesh_id)

    def exchange(source, target, sends, recvs, at):
        return [
            pltpu.make_async_remote_copy(
                src_ref=source(peer), dst_ref=target,
                send_sem=sends.at[at, r], recv_sem=recvs.at[at, r],
                device_id={"sample": peer}, device_id_type=mesh_id,
            )
            for r, peer in enumerate(peers)
        ]

    def forward(p):
        return exchange(lambda peer: send.at[p, turned(peer, block)], recv.at[p, me], f_send, f_recv, p)

    def forward_phi():
        return exchange(lambda peer: phi_send.at[turned(peer, block)], phi_recv.at[me], f_send, f_recv, PLANES)

    def backward(p):
        return exchange(lambda peer: hsend.at[p, peer], hrecv.at[p, slab], b_send, b_recv, p)

    row_id = lax.broadcasted_iota(jnp.int32, (NY, NZ), 0)
    lane_id = lax.broadcasted_iota(jnp.int32, (NY, NZ), 1)
    slab_row = lax.broadcasted_iota(jnp.int32, (ROWS, NZ), 0)
    slab_lane = lax.broadcasted_iota(jnp.int32, (ROWS, NZ), 1)

    def next_row(a):
        return jnp.where(row_id == NY - 1, 0.0, pltpu.roll(a, NY - 1, 0))

    def next_lane(a):
        return jnp.where(lane_id == NZ - 1, 0.0, pltpu.roll(a, NZ - 1, 1))

    def prior_row(a):
        return jnp.where(row_id == 0, 0.0, pltpu.roll(a, 1, 0))

    def prior_lane(a):
        return jnp.where(lane_id == 0, 0.0, pltpu.roll(a, 1, 1))

    def slab_next_row(a, row):
        return jnp.where(slab_row == ROWS - 1, row, pltpu.roll(a, ROWS - 1, 0))

    def slab_next_lane(a):
        return jnp.where(slab_lane == NZ - 1, 0.0, pltpu.roll(a, NZ - 1, 1))

    def slab_prior_row(a):
        return jnp.where(slab_row == 0, 0.0, pltpu.roll(a, 1, 0))

    def slab_prior_lane(a):
        return jnp.where(slab_lane == 0, 0.0, pltpu.roll(a, 1, 1))

    def put_rows(ref, first, at, a):
        for s in range(GROUP - 1):
            ref[s, first + at // ROWS, pl.ds(at % ROWS, 1), :] = a[ROWS * (s + 1):ROWS * (s + 1) + 1, :]

    nothing = jnp.zeros((2, ROWS, NZ), jnp.float32)
    phi_send[GROUP - 1, pl.ds(PAIRS, 2)] = nothing

    @pl.loop(0, PLANES)
    def _(p):
        send[p, GROUP - 1, pl.ds(2 * PAIRS, 2)] = nothing

    for copy in load(0):
        copy.wait()
    for i in range(2):
        for j in range(OWN):
            at = i * OWN + j
            one, two = pot[i, 0, j, 1], pot[i, 0, j, 2]
            send[0, :, at] = one.reshape(GROUP, ROWS, NZ)
            send[0, :, PAIRS + at] = two.reshape(GROUP, ROWS, NZ)
            put_rows(send.at[0], 2 * PAIRS, at, two)
            phi[0, i, j] = pot[i, 0, j, 0]
    recv[0, me] = send[0, slab]
    pl.semaphore_wait(barrier, GROUP + 1)
    for copy in forward(0):
        copy.start()

    @pl.loop(1, PLANES)
    def _(p):
        for copy in load(p):
            copy.wait()

        for i in range(2):
            @pl.loop(0, OWN)
            def _(j):
                phi[p, i, j] = phi[p - 1, i, j] + pot[i, p, j, 0]

    for i in range(2):
        for j in range(OWN):
            at = i * OWN + j
            top = phi[PLANES - 1, i, j]
            phi_send[:, at] = top.reshape(GROUP, ROWS, NZ)
            put_rows(phi_send, PAIRS, at, top)
    phi_recv[me] = phi_send[slab]
    for copy in forward_phi():
        copy.start()

    @pl.loop(0, PLANES - 1)
    def _(k):
        p = PLANES - 1 - k
        for i in range(2):
            for j in range(OWN):
                at = i * OWN + j
                under = phi[p - 1, i, j]
                one = pot[i, p, j, 1] - (next_row(under) - under)
                two = pot[i, p, j, 2] - (next_lane(under) - under)
                send[p, :, at] = one.reshape(GROUP, ROWS, NZ)
                send[p, :, PAIRS + at] = two.reshape(GROUP, ROWS, NZ)
                put_rows(send.at[p], 2 * PAIRS, at, two)
        recv[p, me] = send[p, slab]
        for copy in forward(p):
            copy.start()

    for copy in forward(0):
        copy.wait_recv()
    up = pltpu.make_async_remote_copy(
        src_ref=recv.at[0, :, pl.ds(0, 2 * PAIRS)], dst_ref=upper,
        send_sem=up_send, recv_sem=up_recv, device_id=down_id, device_id_type=mesh_id,
    )
    up.start()
    for copy in material:
        copy.wait()
    psi[...] = jnp.zeros_like(psi)
    for copy in forward_phi():
        copy.wait_recv()
    up.wait_recv()
    last = block == blocks - 1

    @pl.loop(0, GROUP)
    def _(q):
        for at in range(PAIRS):
            top = phi_recv[q, at]
            row = phi_recv[q, PAIRS + at // ROWS, pl.ds(at % ROWS, 1), :]
            one = jnp.where(last, 0.0, upper[q, at])
            two = jnp.where(last, 0.0, upper[q, PAIRS + at])
            recv[PLANES, q, at] = one - (slab_next_row(top, row) - top)
            recv[PLANES, q, PAIRS + at] = two - (slab_next_lane(top) - top)

    down = pltpu.make_async_remote_copy(
        src_ref=hsend.at[PLANES, :, pl.ds(0, PAIRS)], dst_ref=lower,
        send_sem=low_send, recv_sem=low_recv, device_id=up_id, device_id_type=mesh_id,
    )

    def nonlinear(p):
        @pl.loop(0, GROUP)
        def _(q):
            for i in range(2):
                for j in range(OWN):
                    at = i * OWN + j
                    one, two = recv[p, q, at], recv[p, q, PAIRS + at]
                    row = recv[p, q, 2 * PAIRS + at // ROWS, pl.ds(at % ROWS, 1), :]
                    flux[3 * i, q, j] = (slab_next_row(two, row) - two) - (slab_next_lane(one) - one)
                    flux[3 * i + 1, q, j] = two - recv[p + 1, q, PAIRS + at]
                    flux[3 * i + 2, q, j] = recv[p + 1, q, at] - one

        @pl.loop(0, 6)
        def _(pc):
            for t, (kind, orders) in enumerate(CLASSES):
                where = [coef_index(kind, m) for m in orders]
                terms = [flux[pc, c // OWN, c % OWN] for c in where]
                for n in range(FOLDS):
                    wave[n, t, pc] = combine(terms, [factor(kind, m, n) for m in orders])

        density, region = dens[p], regn[p]
        iron = region == 0
        share = jnp.where(iron, density * density * density, 0.0) * jnp.float32(1.0 - iron_floor)
        slope = jnp.where(iron, 3.0 * density * density, 0.0)
        base = jnp.where(region == 1, jnp.float32(magnet_reluct), jnp.float32(1.0))

        def samples(n, total):
            state = [[], [], []]
            adjoint = [[], [], []]
            for pc in range(6):
                ce, co, se, so = (wave[n, t, pc] for t in range(4))
                a, b, d, f = ce + co, ce - co, se + so, se - so
                (state if pc < 3 else adjoint)[pc % 3] = (a + d, a - d, b - f, b + f)
            field = [[], [], []]
            part = None
            for v in range(4):
                s = [state[c][v] for c in range(3)]
                g = [adjoint[c][v] for c in range(3)]
                square = s[0] * s[0] + s[1] * s[1] + s[2] * s[2]
                inner = s[0] * g[0] + s[1] * g[1] + s[2] * g[2]
                r = 1.0 / (square + 1.0)
                t = share * r
                ri = r * inner
                nu = base - t
                mu = (t + t) * ri
                part = ri if part is None else part + ri
                for c in range(3):
                    field[c].append(nu * g[c] + mu * s[c])
            for c in range(3):
                w, x, y, z = field[c]
                a, d = w + x, w - x
                b, f = z + y, z - y
                fold[n, 0, c] = a + b
                fold[n, 1, c] = a - b
                fold[n, 2, c] = d + f
                fold[n, 3, c] = d - f
            ends = (n == 0) | (n == FOLDS - 1)
            return total + part * jnp.where(ends, 0.5, 1.0)

        total = lax.fori_loop(0, FOLDS, samples, jnp.zeros((ROWS, NZ), jnp.float32))
        grad[p] = total * slope * jnp.float32((1.0 - iron_floor) / NT)

        for t, (kind, orders) in enumerate(CLASSES):
            for c in (1, 2, 0):
                terms = [fold[n, t, c] for n in range(FOLDS)]
                for m in orders:
                    scales = [
                        factor(kind, m, n) * (1.0 if 0 < n < FOLDS - 1 else 0.5) * 2.0 / NT
                        for n in range(FOLDS)
                    ]
                    got = combine(terms, scales)
                    at = coef_index(kind, m)
                    q, j = at // OWN, at % OWN
                    old = psi[at]
                    if c == 1:
                        hsend[p + 1, q, j] = got - (slab_prior_row(old) - old)
                    elif c == 2:
                        hsend[p + 1, q, OWN + j] = got - (slab_prior_lane(old) - old)
                    else:
                        hsend[p + 1, q, PAIRS, pl.ds(j, 1), :] = old[ROWS - 1:, :]
                        psi[at] = old + got

    def give_back(p):
        hrecv[p, slab] = hsend[p, me]
        for copy in backward(p):
            copy.start()

    @pl.loop(0, PLANES)
    def _(k):
        p = PLANES - 1 - k

        @pl.when(p > 0)
        def _():
            for copy in forward(p):
                copy.wait_recv()

        nonlinear(p)

        @pl.when(k == 0)
        def _():
            down.start()

        give_back(p + 1)

    down.wait_recv()
    first = block == 0
    for q in range(GROUP):
        for j in range(OWN):
            old = psi[q * OWN + j]
            one = jnp.where(first, 0.0, lower[q, j])
            two = jnp.where(first, 0.0, lower[q, OWN + j])
            hsend[0, q, j] = one - (slab_prior_row(old) - old)
            hsend[0, q, OWN + j] = two - (slab_prior_lane(old) - old)
            hsend[0, q, PAIRS, pl.ds(j, 1), :] = old[ROWS - 1:, :]
    give_back(0)

    swap = pltpu.make_async_remote_copy(
        src_ref=grad, dst_ref=grad_in, send_sem=g_send, recv_sem=g_recv,
        device_id={"sample": lax.rem(me + 2, GROUP)}, device_id_type=mesh_id,
    )
    gradient = pltpu.make_async_copy(grad, grad_hbm, grad_sem)
    swapped = pltpu.make_async_copy(grad_in, grad_hbm, grad_sem)

    @pl.when(odd == 1)
    def _():
        swap.start()

    @pl.when(odd == 0)
    def _():
        gradient.start()

    def store(p):
        return pltpu.make_async_copy(out.at[p], out_hbm.at[:, :, p], out_sems.at[p])

    def field_one(p, j):
        parts = []
        for s in range(GROUP):
            own = hrecv[p, s, j]
            if s:
                row = hrecv[p, s - 1, PAIRS, pl.ds(j, 1), :]
                own = own - jnp.where(slab_row == 0, row, 0.0)
            parts.append(own)
        return jnp.concatenate(parts, axis=0)

    def field_two(p, j):
        return hrecv[p, :, OWN + j].reshape(NY, NZ)

    objective.wait()
    for copy in backward(PLANES):
        copy.wait_recv()

    @pl.loop(0, PLANES)
    def _(k):
        p = PLANES - 1 - k
        for copy in backward(p):
            copy.wait_recv()

        for j in range(OWN):
            one, two = field_one(p + 1, j), field_two(p + 1, j)
            first_part = (prior_lane(one) - one) - (prior_row(two) - two)
            second_part = field_two(p, j) - two
            third_part = one - field_one(p, j)
            for c, part in enumerate((first_part, second_part, third_part)):
                out[p, j, c] = obj[j, c, p] - part
        store(p).start()

    @pl.when(odd == 1)
    def _():
        swap.wait_recv()
        swapped.start()
        swapped.wait()
        swap.wait_send()

    @pl.when(odd == 0)
    def _():
        gradient.wait()

    up.wait_send()
    down.wait_send()
    for copy in forward_phi() + backward(PLANES):
        copy.wait_send()

    @pl.loop(0, PLANES)
    def _(p):
        store(p).wait()
        for copy in forward(p) + backward(p):
            copy.wait_send()


def local(state_hat, adjoint_hat, objective_hat, density, region):
    f32 = jnp.float32
    hbm = pl.BlockSpec(memory_space=pl.ANY)
    dma = pltpu.SemaphoreType.DMA
    links = (PLANES + 1, GROUP - 1)
    return pl.pallas_call(
        kernel,
        out_shape=(
            jax.ShapeDtypeStruct((OWN, 3, PLANES, NY, NZ), f32),
            jax.ShapeDtypeStruct((PLANES, ROWS, NZ), f32),
        ),
        in_specs=[hbm] * 5,
        out_specs=(hbm, hbm),
        scratch_shapes=[
            pltpu.VMEM((2, PLANES, OWN, 3, NY, NZ), f32),
            pltpu.VMEM((PLANES, 2, OWN, NY, NZ), f32),
            pltpu.VMEM((OWN, 3, PLANES, NY, NZ), f32),
            pltpu.VMEM((PLANES, ROWS, NZ), f32),
            pltpu.VMEM((PLANES, ROWS, NZ), jnp.int32),
            pltpu.VMEM((GROUP, 2 * PAIRS, ROWS, NZ), f32),
            pltpu.VMEM((GROUP, PAIRS, ROWS, NZ), f32),
            pltpu.VMEM((PLANES, GROUP, 2 * PAIRS + 2, ROWS, NZ), f32),
            pltpu.VMEM((PLANES + 1, GROUP, 2 * PAIRS + 2, ROWS, NZ), f32),
            pltpu.VMEM((GROUP, PAIRS + 2, ROWS, NZ), f32),
            pltpu.VMEM((GROUP, PAIRS + 2, ROWS, NZ), f32),
            pltpu.VMEM((PLANES + 1, GROUP, PAIRS + 1, ROWS, NZ), f32),
            pltpu.VMEM((PLANES + 1, GROUP, PAIRS + 1, ROWS, NZ), f32),
            pltpu.VMEM((6, GROUP, OWN, ROWS, NZ), f32),
            pltpu.VMEM((FOLDS, 4, 6, ROWS, NZ), f32),
            pltpu.VMEM((FOLDS, 4, 3, ROWS, NZ), f32),
            pltpu.VMEM((NCOEF, ROWS, NZ), f32),
            pltpu.VMEM((PLANES, OWN, 3, NY, NZ), f32),
            pltpu.VMEM((PLANES, ROWS, NZ), f32),
            pltpu.VMEM((PLANES, ROWS, NZ), f32),
            dma((2, PLANES)), dma, dma((2,)), dma, dma, dma, dma,
            dma(links), dma(links), dma(links), dma(links),
            dma, dma, dma((PLANES,)), dma,
        ],
        compiler_params=pltpu.CompilerParams(
            collective_id=0, has_side_effects=True, vmem_limit_bytes=60 * 1024 * 1024
        ),
    )(state_hat, adjoint_hat, objective_hat, density, region)


def solution(mesh):
    in_specs = (
        P("sample", None, "space", None, None),
        P("sample", None, "space", None, None),
        P("sample", None, "space", None, None),
        P("space", None, None),
        P("space", None, None),
    )
    out_specs = (P("sample", None, "space", None, None), P("space", "sample", None))
    return jax.shard_map(local, mesh=mesh, in_specs=in_specs, out_specs=out_specs, check_vma=False)
```

time: 86.2 us -> 67.3 us (0.78)
  Pallas kernels: 81.7 us -> 62.8 us
    pallas_call x1, Pallas kernels: 81.7 us -> 62.8 us  [local(): pl.pallas_call(kernel, out_shape=(jax.ShapeDtypeStruct((OWN, 3, PLANES, N...]
where the time goes in v2:
time: 67.3 us; the launch traced here: 67.1 us
  Pallas kernels  62.8 us (93%)
  local copies, waits for them, and re-layouts  3.66 us (5%)
    pallas_call x1, Pallas kernels, local(): pl.pallas_call(kernel, out_shape=(jax.ShapeDtypeStruct((OWN, 3, PLANES, N...  62.8 us
    unnamed x4, local copies, waits for them, and re-layouts  3.66 us

profile of v2, /device:TPU:1, one launch (start us, length us, event | category | flops | bytes accessed | tf_op | source)
XLA Modules:
  0.0 67.1 jit_solution(1382151967084855416)
XLA Ops:
  0.6 62.8 %shard_map.68 = (f32[5,3,8,32,128]{4,3,2,1,0:T(8,128)}, f32[8,8,128]{2,1,0:T(8,128)}) custom-call(f32[5,3,8,32,128]{4,3,2,1,0:T(8,128)} %state_hbm.1, f32[5,3,8,32,128]{4,3,2,1,0:T(8,128)} %adjoint_hbm.1, f32[5,3,8,32,128]{4,3,2,1,0:T(8,128)} %objective_hbm.1, f32[8,32,128]{2,1,0:T(8,128)} %density_hbm.1, s32[8,32,128]{2,1,0:T(8,128)} %region_hbm.1), custom_call_target="tpu_custom_call" | custom-call | tf_op jit(solution)/shard_map/pallas_call | solution.py:447
  63.4 0.0 copy-start
  63.5 3.0 %copy.9 = f32[5,3,8,32,128]{4,3,2,1,0:T(8,128)} copy(f32[5,3,8,32,128]{4,3,2,1,0:T(8,128)} %get-tuple-element.4) | data formatting | bytes 3932160
  66.5 0.0 copy-done
  66.5 0.6 copy.10
Async XLA Ops:
  63.4 3.1 %copy-start = (f32[8,8,128]{2,1,0:T(8,128)S(1)}, f32[8,8,128]{2,1,0:T(8,128)}, u32[]{:S(2)}) copy-start(f32[8,8,128]{2,1,0:T(8,128)} %get-tuple-element.5) | copy-start | bytes 98308

commit v3 on v2

--- a/solution.py
+++ b/solution.py
@@ -61,11 +61,11 @@
 
 def kernel(
     state_hbm, adjoint_hbm, objective_hbm, density_hbm, region_hbm,
-    out_hbm, grad_hbm,
+    out, grad_out,
     pot, phi, obj, dens, regn, upper, lower, send, recv, phi_send, phi_recv,
-    hsend, hrecv, flux, wave, fold, psi, out, grad, grad_in,
+    hsend, hrecv, flux, wave, fold, psi, grad,
     in_sems, obj_sem, mat_sems, up_send, up_recv, low_send, low_recv,
-    f_send, f_recv, b_send, b_recv, g_send, g_recv, out_sems, grad_sem,
+    f_send, f_recv, b_send, b_recv, g_send, g_recv,
 ):
     me = lax.axis_index("sample")
     block = lax.axis_index("space")
@@ -107,8 +107,15 @@
     barrier = pltpu.get_barrier_semaphore()
     for peer in peers:
         pl.semaphore_signal(barrier, inc=1, device_id={"sample": peer}, device_id_type=mesh_id)
-    for other in (up_id, down_id):
-        pl.semaphore_signal(barrier, inc=1, device_id=other, device_id_type=mesh_id)
+    has_above, has_below = block < blocks - 1, block > 0
+
+    @pl.when(has_above)
+    def _():
+        pl.semaphore_signal(barrier, inc=1, device_id=up_id, device_id_type=mesh_id)
+
+    @pl.when(has_below)
+    def _():
+        pl.semaphore_signal(barrier, inc=1, device_id=down_id, device_id_type=mesh_id)
 
     def exchange(source, target, sends, recvs, at):
         return [
@@ -180,7 +187,7 @@
             put_rows(send.at[0], 2 * PAIRS, at, two)
             phi[0, i, j] = pot[i, 0, j, 0]
     recv[0, me] = send[0, slab]
-    pl.semaphore_wait(barrier, GROUP + 1)
+    pl.semaphore_wait(barrier, GROUP - 1 + has_above.astype(jnp.int32) + has_below.astype(jnp.int32))
     for copy in forward(0):
         copy.start()
 
@@ -226,22 +233,36 @@
         src_ref=recv.at[0, :, pl.ds(0, 2 * PAIRS)], dst_ref=upper,
         send_sem=up_send, recv_sem=up_recv, device_id=down_id, device_id_type=mesh_id,
     )
-    up.start()
+
+    @pl.when(has_below)
+    def _():
+        up.start()
+
+    @pl.when(jnp.logical_not(has_above))
+    def _():
+        upper[...] = jnp.zeros_like(upper)
+
+    @pl.when(jnp.logical_not(has_below))
+    def _():
+        lower[...] = jnp.zeros_like(lower)
+
     for copy in material:
         copy.wait()
     psi[...] = jnp.zeros_like(psi)
     for copy in forward_phi():
         copy.wait_recv()
-    up.wait_recv()
-    last = block == blocks - 1
+
+    @pl.when(has_above)
+    def _():
+        up.wait_recv()
 
     @pl.loop(0, GROUP)
     def _(q):
         for at in range(PAIRS):
             top = phi_recv[q, at]
             row = phi_recv[q, PAIRS + at // ROWS, pl.ds(at % ROWS, 1), :]
-            one = jnp.where(last, 0.0, upper[q, at])
-            two = jnp.where(last, 0.0, upper[q, PAIRS + at])
+            one = upper[q, at]
+            two = upper[q, PAIRS + at]
             recv[PLANES, q, at] = one - (slab_next_row(top, row) - top)
             recv[PLANES, q, PAIRS + at] = two - (slab_next_lane(top) - top)
 
@@ -348,30 +369,30 @@
 
         nonlinear(p)
 
-        @pl.when(k == 0)
+        @pl.when((k == 0) & has_above)
         def _():
             down.start()
 
         give_back(p + 1)
 
-    down.wait_recv()
-    first = block == 0
+    @pl.when(has_below)
+    def _():
+        down.wait_recv()
+
     for q in range(GROUP):
         for j in range(OWN):
             old = psi[q * OWN + j]
-            one = jnp.where(first, 0.0, lower[q, j])
-            two = jnp.where(first, 0.0, lower[q, OWN + j])
+            one = lower[q, j]
+            two = lower[q, OWN + j]
             hsend[0, q, j] = one - (slab_prior_row(old) - old)
             hsend[0, q, OWN + j] = two - (slab_prior_lane(old) - old)
             hsend[0, q, PAIRS, pl.ds(j, 1), :] = old[ROWS - 1:, :]
     give_back(0)
 
     swap = pltpu.make_async_remote_copy(
-        src_ref=grad, dst_ref=grad_in, send_sem=g_send, recv_sem=g_recv,
+        src_ref=grad, dst_ref=grad_out, send_sem=g_send, recv_sem=g_recv,
         device_id={"sample": lax.rem(me + 2, GROUP)}, device_id_type=mesh_id,
     )
-    gradient = pltpu.make_async_copy(grad, grad_hbm, grad_sem)
-    swapped = pltpu.make_async_copy(grad_in, grad_hbm, grad_sem)
 
     @pl.when(odd == 1)
     def _():
@@ -379,10 +400,7 @@
 
     @pl.when(odd == 0)
     def _():
-        gradient.start()
-
-    def store(p):
-        return pltpu.make_async_copy(out.at[p], out_hbm.at[:, :, p], out_sems.at[p])
+        grad_out[...] = grad[...]
 
     def field_one(p, j):
         parts = []
@@ -413,30 +431,36 @@
             second_part = field_two(p, j) - two
             third_part = one - field_one(p, j)
             for c, part in enumerate((first_part, second_part, third_part)):
-                out[p, j, c] = obj[j, c, p] - part
-        store(p).start()
+                out[j, c, p] = obj[j, c, p] - part
 
     @pl.when(odd == 1)
     def _():
-        swap.wait_recv()
-        swapped.start()
-        swapped.wait()
-        swap.wait_send()
-
-    @pl.when(odd == 0)
-    def _():
-        gradient.wait()
-
-    up.wait_send()
-    down.wait_send()
+        swap.wait()
+
+    @pl.when(has_below)
+    def _():
+        up.wait_send()
+
+    @pl.when(has_above)
+    def _():
+        down.wait_send()
+
     for copy in forward_phi() + backward(PLANES):
         copy.wait_send()
 
     @pl.loop(0, PLANES)
     def _(p):
-        store(p).wait()
         for copy in forward(p) + backward(p):
             copy.wait_send()
+
+
+def write_out(held, held_grad, out_hbm, grad_hbm, sems):
+    copies = [pltpu.make_async_copy(held.at[j], out_hbm.at[j], sems.at[j]) for j in range(OWN)]
+    copies.append(pltpu.make_async_copy(held_grad, grad_hbm, sems.at[OWN]))
+    for copy in copies:
+        copy.start()
+    for copy in copies:
+        copy.wait()
 
 
 def local(state_hat, adjoint_hat, objective_hat, density, region):
@@ -444,14 +468,14 @@
     hbm = pl.BlockSpec(memory_space=pl.ANY)
     dma = pltpu.SemaphoreType.DMA
     links = (PLANES + 1, GROUP - 1)
-    return pl.pallas_call(
+    residual = (OWN, 3, PLANES, NY, NZ)
+    gradient = (PLANES, ROWS, NZ)
+    vmem = pl.BlockSpec(memory_space=pltpu.VMEM)
+    held = pl.pallas_call(
         kernel,
-        out_shape=(
-            jax.ShapeDtypeStruct((OWN, 3, PLANES, NY, NZ), f32),
-            jax.ShapeDtypeStruct((PLANES, ROWS, NZ), f32),
-        ),
+        out_shape=(pltpu.VMEM(residual, f32), pltpu.VMEM(gradient, f32)),
         in_specs=[hbm] * 5,
-        out_specs=(hbm, hbm),
+        out_specs=(vmem, vmem),
         scratch_shapes=[
             pltpu.VMEM((2, PLANES, OWN, 3, NY, NZ), f32),
             pltpu.VMEM((PLANES, 2, OWN, NY, NZ), f32),
@@ -470,17 +494,23 @@
             pltpu.VMEM((FOLDS, 4, 6, ROWS, NZ), f32),
             pltpu.VMEM((FOLDS, 4, 3, ROWS, NZ), f32),
             pltpu.VMEM((NCOEF, ROWS, NZ), f32),
-            pltpu.VMEM((PLANES, OWN, 3, NY, NZ), f32),
-            pltpu.VMEM((PLANES, ROWS, NZ), f32),
             pltpu.VMEM((PLANES, ROWS, NZ), f32),
             dma((2, PLANES)), dma, dma((2,)), dma, dma, dma, dma,
             dma(links), dma(links), dma(links), dma(links),
-            dma, dma, dma((PLANES,)), dma,
+            dma, dma,
         ],
         compiler_params=pltpu.CompilerParams(
             collective_id=0, has_side_effects=True, vmem_limit_bytes=60 * 1024 * 1024
         ),
     )(state_hat, adjoint_hat, objective_hat, density, region)
+    return pl.pallas_call(
+        write_out,
+        out_shape=(jax.ShapeDtypeStruct(residual, f32), jax.ShapeDtypeStruct(gradient, f32)),
+        in_specs=[vmem, vmem],
+        out_specs=(hbm, hbm),
+        scratch_shapes=[dma((OWN + 1,))],
+        compiler_params=pltpu.CompilerParams(vmem_limit_bytes=1024 * 1024),
+    )(*held)
 
 
 def solution(mesh):

time: 67.3 us -> 59.9 us (0.89)
  the two profiles are of different devices: /device:TPU:1 before, /device:TPU:105 now
where the time goes in v3:
time: 59.9 us; the launch traced here: 59.8 us
  Pallas kernels  59.2 us (99%)
  between operations  0.64 us (1%)
    pallas_call x1, Pallas kernels, local(): pl.pallas_call(kernel, out_shape=(pltpu.VMEM(residual, f32), pltpu.VMEM(g...  57.9 us
    pallas_call x1, Pallas kernels, local(): pl.pallas_call(write_out, out_shape=(jax.ShapeDtypeStruct(residual, f32),...  1.32 us

profile of v3, /device:TPU:105, one launch (start us, length us, event | category | flops | bytes accessed | tf_op | source)
XLA Modules:
  0.0 59.8 jit_solution(5715825795489160752)
XLA Ops:
  0.6 57.9 %shard_map.68 = (f32[5,3,8,32,128]{4,3,2,1,0:T(8,128)S(1)}, f32[8,8,128]{2,1,0:T(8,128)S(1)}) custom-call(f32[5,3,8,32,128]{4,3,2,1,0:T(8,128)} %state_hbm.1, f32[5,3,8,32,128]{4,3,2,1,0:T(8,128)} %adjoint_hbm.1, f32[5,3,8,32,128]{4,3,2,1,0:T(8,128)} %objective_hbm.1, f32[8,32,128]{2,1,0:T(8,128)} %density_hbm.1, s32[8,32,128]{2,1,0:T(8,128)} %region_hbm.1), custom_call_target="tpu_custom_call" | custom-call | tf_op jit(solution)/shard_map/pallas_call | solution.py:474
  58.5 1.3 %shard_map.69 = (f32[5,3,8,32,128]{4,3,2,1,0:T(8,128)}, f32[8,8,128]{2,1,0:T(8,128)}) custom-call(f32[5,3,8,32,128]{4,3,2,1,0:T(8,128)S(1)} %get-tuple-element.4.held, f32[8,8,128]{2,1,0:T(8,128)S(1)} %get-tuple-element.5.held_grad), custom_call_target="tpu_custom_call" | custom-call | tf_op jit(solution)/shard_map/pallas_call | solution.py:506

commit v4 on v3

v4 whole, which is shorter than its diff:
```python
import math

import jax
import jax.numpy as jnp
from jax import lax
from jax.experimental import pallas as pl
from jax.experimental.pallas import tpu as pltpu
from jax.sharding import PartitionSpec as P

NT = 40
NCOEF = 20
NY = 32
NZ = 128
PLANES = 8
GROUP = 4
OWN = NCOEF // GROUP
ROWS = NY // GROUP
FOLDS = NT // 4 + 1
PAIRS = 2 * OWN
RUN = 4

magnet_reluct = 0.95
iron_floor = 0.05

CLASSES = (
    ("cos", (2, 4, 6, 8, 10)),
    ("cos", (1, 3, 5, 7, 9)),
    ("sin", (2, 4, 6, 8, 10)),
    ("sin", (1, 3, 5, 7, 9)),
)


def coef_index(kind, order):
    return 2 * (order - 1) + (0 if kind == "cos" else 1)


def factor(kind, order, n):
    turn = (n * order) % NT
    quarter = NT // 4
    if kind == "sin":
        turn = (turn - quarter) % NT
    if turn % quarter == 0:
        return (1.0, 0.0, -1.0, 0.0)[turn // quarter]
    return math.cos(2.0 * math.pi * turn / NT)


def combine(terms, constants):
    total = None
    for term, constant in zip(terms, constants):
        if constant == 0.0:
            continue
        if constant == 1.0:
            piece = term
        elif constant == -1.0:
            piece = -term
        else:
            piece = term * jnp.float32(constant)
        total = piece if total is None else total + piece
    return jnp.zeros_like(terms[0]) if total is None else total


def kernel(
    state_hbm, adjoint_hbm, objective_hbm, density_hbm, region_hbm,
    out, grad_out,
    pot, phi, obj, dens, regn, upper, lower, send, recv, phi_send, phi_recv, edge,
    hsend, hrecv, flux, wave, fold, psi, psi_edge, fix, grad,
    in_sems, obj_sem, mat_sems, own_sems, up_send, up_recv, low_send, low_recv,
    f_send, f_recv, b_send, b_recv, e_send, e_recv, c_send, c_recv,
    s_send, s_recv, x_send, x_recv, g_send, g_recv, ready,
):
    me = lax.axis_index("sample")
    block = lax.axis_index("space")
    blocks = lax.axis_size("space")
    above = lax.rem(block + 1, blocks)
    below = lax.rem(block + blocks - 1, blocks)
    has_above, has_below = block < blocks - 1, block > 0
    mesh_id = pl.DeviceIdType.MESH

    def turned(index, where):
        return lax.rem(index + 2 * lax.rem(where // RUN, 2), GROUP)

    swaps = lax.rem(block // RUN, 2) == 1
    slab = turned(me, block)
    odd_slab = lax.rem(me, 2) == 1
    even_slab = jnp.logical_not(odd_slab)
    partner = me + 1 - 2 * lax.rem(me, 2)
    middle = turned(1, block)
    is_middle = me == middle
    off_middle = me != middle
    up_id = {"space": above, "sample": turned(slab, above)}
    down_id = {"space": below, "sample": turned(slab, below)}
    peers = [lax.rem(me + r, GROUP) for r in (2, 3, 1)]
    arguments = (state_hbm, adjoint_hbm)

    def to_sample(source, target, send_sem, recv_sem, peer):
        return pltpu.make_async_remote_copy(
            src_ref=source, dst_ref=target, send_sem=send_sem, recv_sem=recv_sem,
            device_id={"sample": peer}, device_id_type=mesh_id,
        )

    barrier = pltpu.get_barrier_semaphore()
    for peer in peers:
        pl.semaphore_signal(barrier, inc=1, device_id={"sample": peer}, device_id_type=mesh_id)

    @pl.when(has_below)
    def _():
        pl.semaphore_signal(barrier, inc=1, device_id=down_id, device_id_type=mesh_id)

    def slab_rows(s):
        return pl.ds(pl.multiple_of(s * ROWS, ROWS), ROWS)

    def load(p):
        return [
            pltpu.make_async_copy(ref.at[:, :, p], pot.at[i, p], in_sems.at[i, p])
            for i, ref in enumerate(arguments)
        ]

    own = [
        pltpu.make_async_copy(
            ref.at[:, pl.ds(1, 2), 0, slab_rows(slab)], recv.at[0, me, pl.ds(i * OWN, OWN)], own_sems.at[i]
        )
        for i, ref in enumerate(arguments)
    ]
    for copy in own:
        copy.start()

    @pl.loop(0, PLANES)
    def _(p):
        for copy in load(p):
            copy.start()

    material = [
        pltpu.make_async_copy(density_hbm.at[:, slab_rows(slab)], dens, mat_sems.at[0]),
        pltpu.make_async_copy(region_hbm.at[:, slab_rows(slab)], regn, mat_sems.at[1]),
    ]
    for copy in material:
        copy.start()
    objective = pltpu.make_async_copy(objective_hbm, obj, obj_sem)
    objective.start()

    def forward_first():
        return [
            to_sample(
                ref.at[:, pl.ds(1, 2), 0, slab_rows(turned(peer, block))],
                recv.at[0, me, pl.ds(i * OWN, OWN)],
                f_send.at[i * (PLANES + 1), r], f_recv.at[i * (PLANES + 1), r], peer,
            )
            for r, peer in enumerate(peers)
            for i, ref in enumerate(arguments)
        ]

    def forward(p):
        return [
            to_sample(
                send.at[p, turned(peer, block)], recv.at[p, me], f_send.at[p, r], f_recv.at[p, r], peer
            )
            for r, peer in enumerate(peers)
        ]

    def forward_phi():
        return [
            to_sample(
                phi_send.at[turned(peer, block)], phi_recv.at[me],
                f_send.at[PLANES, r], f_recv.at[PLANES, r], peer,
            )
            for r, peer in enumerate(peers)
        ]

    def backward(p):
        return [
            to_sample(hsend.at[p, peer], hrecv.at[p, slab], b_send.at[p, r], b_recv.at[p, r], peer)
            for r, peer in enumerate(peers)
        ]

    top_row, end_row = pl.ds(0, 1), pl.ds(ROWS - 1, 1)

    def middle_row(p, q):
        source = send.at[p, 2, :, 1, top_row]
        return to_sample(source, edge.at[p, q, :, top_row], e_send.at[p], e_recv.at[p, q], middle)

    def middle_phi(q):
        source = phi_send.at[2, :, top_row]
        return to_sample(source, edge.at[PLANES, q, :, top_row], e_send.at[PLANES], e_recv.at[PLANES, q], middle)

    def chip_row(p):
        return to_sample(recv.at[p, :, :, 1, top_row], edge.at[p, :, :, top_row], c_send.at[p], c_recv.at[p], partner)

    def chip_phi():
        return to_sample(
            phi_recv.at[:, :, top_row], edge.at[PLANES, :, :, top_row],
            c_send.at[PLANES], c_recv.at[PLANES], partner,
        )

    def psi_row(p):
        return to_sample(psi.at[p, :, end_row], psi_edge.at[p, :, end_row], s_send.at[p], s_recv.at[p], partner)

    def fix_row(p):
        return [
            to_sample(psi.at[p, pl.ds(peer * OWN, OWN), end_row], fix.at[p, :, end_row], x_send.at[p, r], x_recv.at[p], peer)
            for r, peer in enumerate(peers)
        ]

    row_id = lax.broadcasted_iota(jnp.int32, (NY, NZ), 0)
    lane_id = lax.broadcasted_iota(jnp.int32, (NY, NZ), 1)
    slab_row = lax.broadcasted_iota(jnp.int32, (ROWS, NZ), 0)
    slab_lane = lax.broadcasted_iota(jnp.int32, (ROWS, NZ), 1)

    def next_row(a):
        return jnp.where(row_id == NY - 1, 0.0, pltpu.roll(a, NY - 1, 0))

    def next_lane(a):
        return jnp.where(lane_id == NZ - 1, 0.0, pltpu.roll(a, NZ - 1, 1))

    def prior_row(a):
        return jnp.where(row_id == 0, 0.0, pltpu.roll(a, 1, 0))

    def prior_lane(a):
        return jnp.where(lane_id == 0, 0.0, pltpu.roll(a, 1, 1))

    def slab_next_row(a, row):
        return jnp.where(slab_row == ROWS - 1, row, pltpu.roll(a, ROWS - 1, 0))

    def slab_next_lane(a):
        return jnp.where(slab_lane == NZ - 1, 0.0, pltpu.roll(a, NZ - 1, 1))

    def slab_prior_row(a, row):
        return jnp.where(slab_row == 0, row, pltpu.roll(a, 1, 0))

    def slab_prior_lane(a):
        return jnp.where(slab_lane == 0, 0.0, pltpu.roll(a, 1, 1))

    pl.semaphore_wait(barrier, GROUP - 1 + has_above.astype(jnp.int32))
    for copy in forward_first():
        copy.start()

    @pl.when(has_above)
    def _():
        pl.semaphore_signal(ready, inc=1, device_id=up_id, device_id_type=mesh_id)

    for copy in load(0):
        copy.wait()
    for i in range(2):
        for j in range(OWN):
            phi[0, i, j] = pot[i, 0, j, 0]
            send[0, 2, i * OWN + j, 1] = pot[i, 0, j, 2, pl.ds(2 * ROWS, ROWS), :]

    @pl.loop(1, PLANES)
    def _(p):
        for copy in load(p):
            copy.wait()

        for i in range(2):
            @pl.loop(0, OWN)
            def _(j):
                phi[p, i, j] = phi[p - 1, i, j] + pot[i, p, j, 0]

    for i in range(2):
        for j in range(OWN):
            phi_send[:, i * OWN + j] = phi[PLANES - 1, i, j].reshape(GROUP, ROWS, NZ)
    phi_recv[me] = phi_send[slab]
    for copy in forward_phi():
        copy.start()

    @pl.when(off_middle)
    def _():
        middle_phi(me).start()
        middle_row(0, me).start()

    @pl.when(is_middle)
    def _():
        for ij in range(PAIRS):
            edge[PLANES, me, ij] = phi_send[2, ij]
            edge[0, me, ij] = send[0, 2, ij, 1]

    @pl.loop(0, PLANES - 1)
    def _(k):
        p = PLANES - 1 - k
        for i in range(2):
            for j in range(OWN):
                under = phi[p - 1, i, j]
                one = pot[i, p, j, 1] - (next_row(under) - under)
                two = pot[i, p, j, 2] - (next_lane(under) - under)
                send[p, :, i * OWN + j, 0] = one.reshape(GROUP, ROWS, NZ)
                send[p, :, i * OWN + j, 1] = two.reshape(GROUP, ROWS, NZ)
        for copy in forward(p):
            copy.start()

        @pl.when(off_middle)
        def _():
            middle_row(p, me).start()

        @pl.when(is_middle)
        def _():
            for ij in range(PAIRS):
                edge[p, me, ij] = send[p, 2, ij, 1]

        recv[p, me] = send[p, slab]

    psi[PLANES] = jnp.zeros((NCOEF, ROWS, NZ), jnp.float32)
    psi_edge[PLANES] = jnp.zeros((NCOEF, ROWS, NZ), jnp.float32)
    fix[PLANES] = jnp.zeros((OWN, ROWS, NZ), jnp.float32)

    @pl.when(even_slab)
    def _():
        @pl.loop(0, PLANES)
        def _(p):
            psi_edge[p] = jnp.zeros((NCOEF, ROWS, NZ), jnp.float32)

    @pl.when(slab == GROUP - 1)
    def _():
        @pl.loop(0, PLANES + 1)
        def _(p):
            edge[p] = jnp.zeros((GROUP, PAIRS, ROWS, NZ), jnp.float32)

    @pl.when(jnp.logical_not(has_above))
    def _():
        upper[...] = jnp.zeros_like(upper)

    @pl.when(jnp.logical_not(has_below))
    def _():
        lower[...] = jnp.zeros_like(lower)

    for copy in own:
        copy.wait()
    for copy in forward_first():
        copy.wait_recv()
    up = pltpu.make_async_remote_copy(
        src_ref=recv.at[0], dst_ref=upper,
        send_sem=up_send, recv_sem=up_recv, device_id=down_id, device_id_type=mesh_id,
    )

    @pl.when(has_below)
    def _():
        pl.semaphore_wait(ready, 1)
        up.start()

    for copy in material:
        copy.wait()
    for copy in forward_phi():
        copy.wait_recv()

    @pl.when(odd_slab)
    def _():
        chip_phi().start()
        chip_row(0).start()

    @pl.when(is_middle)
    def _():
        for peer in peers:
            middle_phi(peer).wait_recv()
            middle_row(0, peer).wait_recv()

    @pl.when(even_slab)
    def _():
        chip_phi().wait_recv()
        chip_row(0).wait_recv()

    @pl.when(has_above)
    def _():
        up.wait_recv()

    @pl.loop(0, GROUP)
    def _(q):
        for ij in range(PAIRS):
            top = phi_recv[q, ij]
            row = edge[PLANES, q, ij, top_row, :]
            recv[PLANES, q, ij, 0] = upper[q, ij, 0] - (slab_next_row(top, row) - top)
            recv[PLANES, q, ij, 1] = upper[q, ij, 1] - (slab_next_lane(top) - top)

    down = pltpu.make_async_remote_copy(
        src_ref=hsend.at[PLANES], dst_ref=lower,
        send_sem=low_send, recv_sem=low_recv, device_id=up_id, device_id_type=mesh_id,
    )

    def nonlinear(p):
        @pl.loop(0, GROUP)
        def _(q):
            for i in range(2):
                for j in range(OWN):
                    ij = i * OWN + j
                    one, two = recv[p, q, ij, 0], recv[p, q, ij, 1]
                    row = edge[p, q, ij, top_row, :]
                    flux[3 * i, q, j] = (slab_next_row(two, row) - two) - (slab_next_lane(one) - one)
                    flux[3 * i + 1, q, j] = two - recv[p + 1, q, ij, 1]
                    flux[3 * i + 2, q, j] = recv[p + 1, q, ij, 0] - one

        @pl.loop(0, 6)
        def _(pc):
            for t, (kind, orders) in enumerate(CLASSES):
                where = [coef_index(kind, m) for m in orders]
                terms = [flux[pc, c // OWN, c % OWN] for c in where]
                for n in range(FOLDS):
                    wave[n, t, pc] = combine(terms, [factor(kind, m, n) for m in orders])

        density, region = dens[p], regn[p]
        iron = region == 0
        share = jnp.where(iron, density * density * density, 0.0) * jnp.float32(1.0 - iron_floor)
        slope = jnp.where(iron, 3.0 * density * density, 0.0)
        base = jnp.where(region == 1, jnp.float32(magnet_reluct), jnp.float32(1.0))

        def samples(n, total):
            state = [[], [], []]
            adjoint = [[], [], []]
            for pc in range(6):
                ce, co, se, so = (wave[n, t, pc] for t in range(4))
                a, b, d, f = ce + co, ce - co, se + so, se - so
                (state if pc < 3 else adjoint)[pc % 3] = (a + d, a - d, b - f, b + f)
            field = [[], [], []]
            part = None
            for v in range(4):
                s = [state[c][v] for c in range(3)]
                g = [adjoint[c][v] for c in range(3)]
                square = s[0] * s[0] + s[1] * s[1] + s[2] * s[2]
                inner = s[0] * g[0] + s[1] * g[1] + s[2] * g[2]
                r = 1.0 / (square + 1.0)
                t = share * r
                ri = r * inner
                nu = base - t
                mu = (t + t) * ri
                part = ri if part is None else part + ri
                for c in range(3):
                    field[c].append(nu * g[c] + mu * s[c])
            for c in range(3):
                w, x, y, z = field[c]
                a, d = w + x, w - x
                b, f = z + y, z - y
                fold[n, 0, c] = a + b
                fold[n, 1, c] = a - b
                fold[n, 2, c] = d + f
                fold[n, 3, c] = d - f
            ends = (n == 0) | (n == FOLDS - 1)
            return total + part * jnp.where(ends, 0.5, 1.0)

        total = lax.fori_loop(0, FOLDS, samples, jnp.zeros((ROWS, NZ), jnp.float32))
        grad[p] = total * slope * jnp.float32((1.0 - iron_floor) / NT)

        @pl.when(odd_slab & (p < PLANES - 1))
        def _():
            psi_row(p + 1).wait_recv()

        for t, (kind, orders) in enumerate(CLASSES):
            for c in (1, 2, 0):
                terms = [fold[n, t, c] for n in range(FOLDS)]
                for m in orders:
                    scales = [
                        factor(kind, m, n) * (1.0 if 0 < n < FOLDS - 1 else 0.5) * 2.0 / NT
                        for n in range(FOLDS)
                    ]
                    got = combine(terms, scales)
                    at = coef_index(kind, m)
                    q, j = at // OWN, at % OWN
                    old = psi[p + 1, at]
                    if c == 1:
                        row = psi_edge[p + 1, at, end_row, :]
                        hsend[p + 1, q, j, 0] = got - (slab_prior_row(old, row) - old)
                    elif c == 2:
                        hsend[p + 1, q, j, 1] = got - (slab_prior_lane(old) - old)
                    else:
                        psi[p, at] = old + got

    def give_back(u):
        for copy in backward(u):
            copy.start()

        @pl.when(is_middle & (u < PLANES))
        def _():
            for copy in fix_row(u):
                copy.start()

            fix[u] = psi[u, pl.ds(me * OWN, OWN)]

        hrecv[u, slab] = hsend[u, me]

    @pl.loop(0, PLANES)
    def _(k):
        p = PLANES - 1 - k

        @pl.when(p > 0)
        def _():
            for copy in forward(p):
                copy.wait_recv()

            @pl.when(odd_slab)
            def _():
                chip_row(p).start()

            @pl.when(is_middle)
            def _():
                for peer in peers:
                    middle_row(p, peer).wait_recv()

            @pl.when(even_slab)
            def _():
                chip_row(p).wait_recv()

        nonlinear(p)

        @pl.when(even_slab)
        def _():
            psi_row(p).start()

        @pl.when((k == 0) & has_above)
        def _():
            down.start()

        give_back(p + 1)

    @pl.when(has_below)
    def _():
        down.wait_recv()

    @pl.when(odd_slab)
    def _():
        psi_row(0).wait_recv()

    for q in range(GROUP):
        for j in range(OWN):
            old = psi[0, q * OWN + j]
            row = psi_edge[0, q * OWN + j, end_row, :]
            hsend[0, q, j, 0] = lower[q, j, 0] - (slab_prior_row(old, row) - old)
            hsend[0, q, j, 1] = lower[q, j, 1] - (slab_prior_lane(old) - old)
    give_back(0)

    swap = to_sample(grad, grad_out, g_send, g_recv, lax.rem(me + 2, GROUP))

    @pl.when(swaps)
    def _():
        swap.start()

    @pl.when(jnp.logical_not(swaps))
    def _():
        grad_out[...] = grad[...]

    def arrived(u):
        for copy in backward(u):
            copy.wait_recv()

        @pl.when(off_middle & (u < PLANES))
        def _():
            fix_row(u)[0].wait_recv()

    def field_one(u, j):
        parts = [hrecv[u, s, j, 0] for s in range(GROUP)]
        parts[2] = parts[2] - jnp.where(slab_row == 0, fix[u, j, end_row, :], 0.0)
        return jnp.concatenate(parts, axis=0)

    def field_two(u, j):
        return hrecv[u, :, j, 1].reshape(NY, NZ)

    objective.wait()
    arrived(PLANES)

    @pl.loop(0, PLANES)
    def _(k):
        p = PLANES - 1 - k
        arrived(p)

        for j in range(OWN):
            one, two = field_one(p + 1, j), field_two(p + 1, j)
            first_part = (prior_lane(one) - one) - (prior_row(two) - two)
            second_part = field_two(p, j) - two
            third_part = one - field_one(p, j)
            for c, part in enumerate((first_part, second_part, third_part)):
                out[j, c, p] = obj[j, c, p] - part

    @pl.when(swaps)
    def _():
        swap.wait()

    @pl.when(has_below)
    def _():
        up.wait_send()

    @pl.when(has_above)
    def _():
        down.wait_send()

    for copy in forward_first() + forward_phi() + backward(PLANES):
        copy.wait_send()

    @pl.when(off_middle)
    def _():
        middle_phi(me).wait_send()

    @pl.when(odd_slab)
    def _():
        chip_phi().wait_send()

    @pl.loop(0, PLANES)
    def _(p):
        for copy in backward(p):
            copy.wait_send()

        @pl.when(p > 0)
        def _():
            for copy in forward(p):
                copy.wait_send()

        @pl.when(off_middle)
        def _():
            middle_row(p, me).wait_send()

        @pl.when(odd_slab)
        def _():
            chip_row(p).wait_send()

        @pl.when(even_slab)
        def _():
            psi_row(p).wait_send()

        @pl.when(is_middle)
        def _():
            for copy in fix_row(p):
                copy.wait_send()


def write_out(held, held_grad, out_hbm, grad_hbm, sems):
    copies = [pltpu.make_async_copy(held.at[j], out_hbm.at[j], sems.at[j]) for j in range(OWN)]
    copies.append(pltpu.make_async_copy(held_grad, grad_hbm, sems.at[OWN]))
    for copy in copies:
        copy.start()
    for copy in copies:
        copy.wait()


def local(state_hat, adjoint_hat, objective_hat, density, region):
    f32 = jnp.float32
    hbm = pl.BlockSpec(memory_space=pl.ANY)
    dma = pltpu.SemaphoreType.DMA
    links = (PLANES + 1, GROUP - 1)
    residual = (OWN, 3, PLANES, NY, NZ)
    gradient = (PLANES, ROWS, NZ)
    vmem = pl.BlockSpec(memory_space=pltpu.VMEM)
    held = pl.pallas_call(
        kernel,
        out_shape=(pltpu.VMEM(residual, f32), pltpu.VMEM(gradient, f32)),
        in_specs=[hbm] * 5,
        out_specs=(vmem, vmem),
        scratch_shapes=[
            pltpu.VMEM((2, PLANES, OWN, 3, NY, NZ), f32),
            pltpu.VMEM((PLANES, 2, OWN, NY, NZ), f32),
            pltpu.VMEM((OWN, 3, PLANES, NY, NZ), f32),
            pltpu.VMEM((PLANES, ROWS, NZ), f32),
            pltpu.VMEM((PLANES, ROWS, NZ), jnp.int32),
            pltpu.VMEM((GROUP, PAIRS, 2, ROWS, NZ), f32),
            pltpu.VMEM((GROUP, OWN, 2, ROWS, NZ), f32),
            pltpu.VMEM((PLANES, GROUP, PAIRS, 2, ROWS, NZ), f32),
            pltpu.VMEM((PLANES + 1, GROUP, PAIRS, 2, ROWS, NZ), f32),
            pltpu.VMEM((GROUP, PAIRS, ROWS, NZ), f32),
            pltpu.VMEM((GROUP, PAIRS, ROWS, NZ), f32),
            pltpu.VMEM((PLANES + 1, GROUP, PAIRS, ROWS, NZ), f32),
            pltpu.VMEM((PLANES + 1, GROUP, OWN, 2, ROWS, NZ), f32),
            pltpu.VMEM((PLANES + 1, GROUP, OWN, 2, ROWS, NZ), f32),
            pltpu.VMEM((6, GROUP, OWN, ROWS, NZ), f32),
            pltpu.VMEM((FOLDS, 4, 6, ROWS, NZ), f32),
            pltpu.VMEM((FOLDS, 4, 3, ROWS, NZ), f32),
            pltpu.VMEM((PLANES + 1, NCOEF, ROWS, NZ), f32),
            pltpu.VMEM((PLANES + 1, NCOEF, ROWS, NZ), f32),
            pltpu.VMEM((PLANES + 1, OWN, ROWS, NZ), f32),
            pltpu.VMEM((PLANES, ROWS, NZ), f32),
            dma((2, PLANES)), dma, dma((2,)), dma((2,)), dma, dma, dma, dma,
            dma((PLANES + 2, GROUP - 1)), dma((PLANES + 2, GROUP - 1)),
            dma((PLANES + 1, GROUP - 1)), dma((PLANES + 1, GROUP - 1)),
            dma((PLANES + 1,)), dma((PLANES + 1, GROUP)),
            dma((PLANES + 1,)), dma((PLANES + 1,)),
            dma((PLANES,)), dma((PLANES,)),
            dma((PLANES, GROUP - 1)), dma((PLANES,)),
            dma, dma, pltpu.SemaphoreType.REGULAR,
        ],
        compiler_params=pltpu.CompilerParams(
            collective_id=0, has_side_effects=True, vmem_limit_bytes=60 * 1024 * 1024
        ),
    )(state_hat, adjoint_hat, objective_hat, density, region)
    return pl.pallas_call(
        write_out,
        out_shape=(jax.ShapeDtypeStruct(residual, f32), jax.ShapeDtypeStruct(gradient, f32)),
        in_specs=[vmem, vmem],
        out_specs=(hbm, hbm),
        scratch_shapes=[dma((OWN + 1,))],
        compiler_params=pltpu.CompilerParams(vmem_limit_bytes=1024 * 1024),
    )(*held)


def solution(mesh):
    in_specs = (
        P("sample", None, "space", None, None),
        P("sample", None, "space", None, None),
        P("sample", None, "space", None, None),
        P("space", None, None),
        P("space", None, None),
    )
    out_specs = (P("sample", None, "space", None, None), P("space", "sample", None))
    return jax.shard_map(local, mesh=mesh, in_specs=in_specs, out_specs=out_specs, check_vma=False)
```

time: 59.9 us -> 55.9 us (0.933)
  the two profiles are of different devices: /device:TPU:105 before, /device:TPU:1 now
where the time goes in v4:
time: 55.9 us; the launch traced here: 55.7 us
  Pallas kernels  55.1 us (99%)
  between operations  0.64 us (1%)
    pallas_call x1, Pallas kernels, local(): pl.pallas_call(kernel, out_shape=(pltpu.VMEM(residual, f32), pltpu.VMEM(g...  53.8 us
    pallas_call x1, Pallas kernels, local(): pl.pallas_call(write_out, out_shape=(jax.ShapeDtypeStruct(residual, f32),...  1.32 us

profile of v4, /device:TPU:1, one launch (start us, length us, event | category | flops | bytes accessed | tf_op | source)
XLA Modules:
  0.0 55.7 jit_solution(7200191300878344912)
XLA Ops:
  0.6 53.8 %shard_map.68 = (f32[5,3,8,32,128]{4,3,2,1,0:T(8,128)S(1)}, f32[8,8,128]{2,1,0:T(8,128)S(1)}) custom-call(f32[5,3,8,32,128]{4,3,2,1,0:T(8,128)} %state_hbm.1, f32[5,3,8,32,128]{4,3,2,1,0:T(8,128)} %adjoint_hbm.1, f32[5,3,8,32,128]{4,3,2,1,0:T(8,128)} %objective_hbm.1, f32[8,32,128]{2,1,0:T(8,128)} %density_hbm.1, s32[8,32,128]{2,1,0:T(8,128)} %region_hbm.1), custom_call_target="tpu_custom_call" | custom-call | tf_op jit(solution)/shard_map/pallas_call | solution.py:634
  54.4 1.3 %shard_map.69 = (f32[5,3,8,32,128]{4,3,2,1,0:T(8,128)}, f32[8,8,128]{2,1,0:T(8,128)}) custom-call(f32[5,3,8,32,128]{4,3,2,1,0:T(8,128)S(1)} %get-tuple-element.4.held, f32[8,8,128]{2,1,0:T(8,128)S(1)} %get-tuple-element.5.held_grad), custom_call_target="tpu_custom_call" | custom-call | tf_op jit(solution)/shard_map/pallas_call | solution.py:674

commit v5 on v4

--- a/solution.py
+++ b/solution.py
@@ -62,8 +62,8 @@
 def kernel(
     state_hbm, adjoint_hbm, objective_hbm, density_hbm, region_hbm,
     out, grad_out,
-    pot, phi, obj, dens, regn, upper, lower, send, recv, phi_send, phi_recv, edge,
-    hsend, hrecv, flux, wave, fold, psi, psi_edge, fix, grad,
+    pot, phi, obj, dens, regn, upper, send, recv, phi_send, phi_recv, edge,
+    bsend, brecv, zsend, zrecv, flux, wave, fold, field, field_edge, fix, below_sum, grad,
     in_sems, obj_sem, mat_sems, own_sems, up_send, up_recv, low_send, low_recv,
     f_send, f_recv, b_send, b_recv, e_send, e_recv, c_send, c_recv,
     s_send, s_recv, x_send, x_recv, g_send, g_recv, ready,
@@ -89,7 +89,7 @@
     off_middle = me != middle
     up_id = {"space": above, "sample": turned(slab, above)}
     down_id = {"space": below, "sample": turned(slab, below)}
-    peers = [lax.rem(me + r, GROUP) for r in (2, 3, 1)]
+    peers = [lax.rem(me + 2, GROUP), lax.rem(partner + 2, GROUP), partner]
     arguments = (state_hbm, adjoint_hbm)
 
     def to_sample(source, target, send_sem, recv_sem, peer):
@@ -168,7 +168,13 @@
 
     def backward(p):
         return [
-            to_sample(hsend.at[p, peer], hrecv.at[p, slab], b_send.at[p, r], b_recv.at[p, r], peer)
+            to_sample(bsend.at[p, peer], brecv.at[p, slab], b_send.at[p, r], b_recv.at[p, r], peer)
+            for r, peer in enumerate(peers)
+        ]
+
+    def backward_zero():
+        return [
+            to_sample(zsend.at[peer], zrecv.at[slab], b_send.at[PLANES, r], b_recv.at[PLANES, r], peer)
             for r, peer in enumerate(peers)
         ]
 
@@ -191,12 +197,21 @@
             c_send.at[PLANES], c_recv.at[PLANES], partner,
         )
 
-    def psi_row(p):
-        return to_sample(psi.at[p, :, end_row], psi_edge.at[p, :, end_row], s_send.at[p], s_recv.at[p], partner)
+    def last_rows(p, some):
+        if isinstance(p, int) and p == PLANES:
+            return field.at[PLANES, 2, some, end_row]
+        return field.at[p + 1, 0, some, end_row]
+
+    def field_row(p):
+        return to_sample(
+            last_rows(p, pl.ds(0, NCOEF)), field_edge.at[p, :, end_row], s_send.at[p], s_recv.at[p], partner
+        )
 
     def fix_row(p):
         return [
-            to_sample(psi.at[p, pl.ds(peer * OWN, OWN), end_row], fix.at[p, :, end_row], x_send.at[p, r], x_recv.at[p], peer)
+            to_sample(
+                last_rows(p, pl.ds(peer * OWN, OWN)), fix.at[p, :, end_row], x_send.at[p, r], x_recv.at[p], peer
+            )
             for r, peer in enumerate(peers)
         ]
 
@@ -296,15 +311,11 @@
 
         recv[p, me] = send[p, slab]
 
-    psi[PLANES] = jnp.zeros((NCOEF, ROWS, NZ), jnp.float32)
-    psi_edge[PLANES] = jnp.zeros((NCOEF, ROWS, NZ), jnp.float32)
-    fix[PLANES] = jnp.zeros((OWN, ROWS, NZ), jnp.float32)
-
     @pl.when(even_slab)
     def _():
-        @pl.loop(0, PLANES)
+        @pl.loop(0, PLANES + 1)
         def _(p):
-            psi_edge[p] = jnp.zeros((NCOEF, ROWS, NZ), jnp.float32)
+            field_edge[p] = jnp.zeros((NCOEF, ROWS, NZ), jnp.float32)
 
     @pl.when(slab == GROUP - 1)
     def _():
@@ -318,7 +329,7 @@
 
     @pl.when(jnp.logical_not(has_below))
     def _():
-        lower[...] = jnp.zeros_like(lower)
+        field[0, pl.ds(1, 2)] = jnp.zeros((2, NCOEF, ROWS, NZ), jnp.float32)
 
     for copy in own:
         copy.wait()
@@ -368,7 +379,7 @@
             recv[PLANES, q, ij, 1] = upper[q, ij, 1] - (slab_next_lane(top) - top)
 
     down = pltpu.make_async_remote_copy(
-        src_ref=hsend.at[PLANES], dst_ref=lower,
+        src_ref=field.at[PLANES, pl.ds(1, 2)], dst_ref=field.at[0, pl.ds(1, 2)],
         send_sem=low_send, recv_sem=low_recv, device_id=up_id, device_id_type=mesh_id,
     )
 
@@ -405,7 +416,7 @@
                 ce, co, se, so = (wave[n, t, pc] for t in range(4))
                 a, b, d, f = ce + co, ce - co, se + so, se - so
                 (state if pc < 3 else adjoint)[pc % 3] = (a + d, a - d, b - f, b + f)
-            field = [[], [], []]
+            values = [[], [], []]
             part = None
             for v in range(4):
                 s = [state[c][v] for c in range(3)]
@@ -419,9 +430,9 @@
                 mu = (t + t) * ri
                 part = ri if part is None else part + ri
                 for c in range(3):
-                    field[c].append(nu * g[c] + mu * s[c])
+                    values[c].append(nu * g[c] + mu * s[c])
             for c in range(3):
-                w, x, y, z = field[c]
+                w, x, y, z = values[c]
                 a, d = w + x, w - x
                 b, f = z + y, z - y
                 fold[n, 0, c] = a + b
@@ -434,42 +445,64 @@
         total = lax.fori_loop(0, FOLDS, samples, jnp.zeros((ROWS, NZ), jnp.float32))
         grad[p] = total * slope * jnp.float32((1.0 - iron_floor) / NT)
 
-        @pl.when(odd_slab & (p < PLANES - 1))
-        def _():
-            psi_row(p + 1).wait_recv()
-
         for t, (kind, orders) in enumerate(CLASSES):
-            for c in (1, 2, 0):
+            for c in range(3):
                 terms = [fold[n, t, c] for n in range(FOLDS)]
                 for m in orders:
                     scales = [
                         factor(kind, m, n) * (1.0 if 0 < n < FOLDS - 1 else 0.5) * 2.0 / NT
                         for n in range(FOLDS)
                     ]
-                    got = combine(terms, scales)
-                    at = coef_index(kind, m)
-                    q, j = at // OWN, at % OWN
-                    old = psi[p + 1, at]
-                    if c == 1:
-                        row = psi_edge[p + 1, at, end_row, :]
-                        hsend[p + 1, q, j, 0] = got - (slab_prior_row(old, row) - old)
-                    elif c == 2:
-                        hsend[p + 1, q, j, 1] = got - (slab_prior_lane(old) - old)
-                    else:
-                        psi[p, at] = old + got
-
-    def give_back(u):
-        for copy in backward(u):
+                    field[p + 1, c, coef_index(kind, m)] = combine(terms, scales)
+
+    def give_back(p):
+        @pl.when(odd_slab)
+        def _():
+            field_row(p).wait_recv()
+
+        @pl.when(is_middle)
+        def _():
+            for copy in fix_row(p):
+                copy.start()
+
+            fix[p] = field[p + 1, 0, pl.ds(me * OWN, OWN)]
+
+        @pl.loop(0, GROUP)
+        def _(q):
+            for j in range(OWN):
+                at = q * OWN + j
+                zero, one, two = (field[p + 1, c, at] for c in range(3))
+                row = field_edge[p, at, end_row, :]
+                bsend[p, q, j, 0] = (field[p, 2, at] - two) - (slab_prior_lane(zero) - zero)
+                bsend[p, q, j, 1] = (slab_prior_row(zero, row) - zero) - (field[p, 1, at] - one)
+
+        for copy in backward(p):
             copy.start()
-
-        @pl.when(is_middle & (u < PLANES))
-        def _():
-            for copy in fix_row(u):
+        brecv[p, slab] = bsend[p, me]
+
+    def give_back_zero():
+        @pl.when(odd_slab)
+        def _():
+            field_row(PLANES).wait_recv()
+
+        @pl.when(is_middle)
+        def _():
+            for copy in fix_row(PLANES):
                 copy.start()
 
-            fix[u] = psi[u, pl.ds(me * OWN, OWN)]
-
-        hrecv[u, slab] = hsend[u, me]
+            fix[PLANES] = field[PLANES, 2, pl.ds(me * OWN, OWN)]
+
+        @pl.loop(0, GROUP)
+        def _(q):
+            for j in range(OWN):
+                at = q * OWN + j
+                one, two = field[PLANES, 1, at], field[PLANES, 2, at]
+                row = field_edge[PLANES, at, end_row, :]
+                zsend[q, j] = (slab_prior_lane(one) - one) - (slab_prior_row(two, row) - two)
+
+        for copy in backward_zero():
+            copy.start()
+        zrecv[slab] = zsend[me]
 
     @pl.loop(0, PLANES)
     def _(k):
@@ -497,28 +530,28 @@
 
         @pl.when(even_slab)
         def _():
-            psi_row(p).start()
-
-        @pl.when((k == 0) & has_above)
-        def _():
-            down.start()
-
-        give_back(p + 1)
+            field_row(p).start()
+
+        @pl.when(k == 0)
+        def _():
+            @pl.when(even_slab)
+            def _():
+                field_row(PLANES).start()
+
+            @pl.when(has_above)
+            def _():
+                down.start()
+
+            give_back_zero()
+
+        @pl.when(k > 0)
+        def _():
+            give_back(p + 1)
 
     @pl.when(has_below)
     def _():
         down.wait_recv()
 
-    @pl.when(odd_slab)
-    def _():
-        psi_row(0).wait_recv()
-
-    for q in range(GROUP):
-        for j in range(OWN):
-            old = psi[0, q * OWN + j]
-            row = psi_edge[0, q * OWN + j, end_row, :]
-            hsend[0, q, j, 0] = lower[q, j, 0] - (slab_prior_row(old, row) - old)
-            hsend[0, q, j, 1] = lower[q, j, 1] - (slab_prior_lane(old) - old)
     give_back(0)
 
     swap = to_sample(grad, grad_out, g_send, g_recv, lax.rem(me + 2, GROUP))
@@ -531,37 +564,39 @@
     def _():
         grad_out[...] = grad[...]
 
-    def arrived(u):
-        for copy in backward(u):
-            copy.wait_recv()
-
-        @pl.when(off_middle & (u < PLANES))
-        def _():
-            fix_row(u)[0].wait_recv()
-
-    def field_one(u, j):
-        parts = [hrecv[u, s, j, 0] for s in range(GROUP)]
-        parts[2] = parts[2] - jnp.where(slab_row == 0, fix[u, j, end_row, :], 0.0)
+    def fixed(parts, p, j, sign):
+        row = jnp.where(slab_row == 0, fix[p, j, end_row, :], 0.0)
+        parts[2] = parts[2] + row if sign > 0 else parts[2] - row
         return jnp.concatenate(parts, axis=0)
 
-    def field_two(u, j):
-        return hrecv[u, :, j, 1].reshape(NY, NZ)
-
     objective.wait()
-    arrived(PLANES)
+    for copy in backward_zero():
+        copy.wait_recv()
+
+    @pl.when(off_middle)
+    def _():
+        fix_row(PLANES)[0].wait_recv()
+
+    for j in range(OWN):
+        below_sum[j] = fixed([zrecv[q, j] for q in range(GROUP)], PLANES, j, -1)
 
     @pl.loop(0, PLANES)
     def _(k):
         p = PLANES - 1 - k
-        arrived(p)
+        for copy in backward(p):
+            copy.wait_recv()
+
+        @pl.when(off_middle)
+        def _():
+            fix_row(p)[0].wait_recv()
 
         for j in range(OWN):
-            one, two = field_one(p + 1, j), field_two(p + 1, j)
-            first_part = (prior_lane(one) - one) - (prior_row(two) - two)
-            second_part = field_two(p, j) - two
-            third_part = one - field_one(p, j)
-            for c, part in enumerate((first_part, second_part, third_part)):
+            zero = below_sum[j]
+            one = brecv[p, :, j, 0].reshape(NY, NZ)
+            two = fixed([brecv[p, q, j, 1] for q in range(GROUP)], p, j, 1)
+            for c, part in enumerate((zero, one, two)):
                 out[j, c, p] = obj[j, c, p] - part
+            below_sum[j] = zero - (prior_row(one) - one) - (prior_lane(two) - two)
 
     @pl.when(swaps)
     def _():
@@ -575,7 +610,7 @@
     def _():
         down.wait_send()
 
-    for copy in forward_first() + forward_phi() + backward(PLANES):
+    for copy in forward_first() + forward_phi() + backward_zero():
         copy.wait_send()
 
     @pl.when(off_middle)
@@ -585,6 +620,15 @@
     @pl.when(odd_slab)
     def _():
         chip_phi().wait_send()
+
+    @pl.when(even_slab)
+    def _():
+        field_row(PLANES).wait_send()
+
+    @pl.when(is_middle)
+    def _():
+        for copy in fix_row(PLANES):
+            copy.wait_send()
 
     @pl.loop(0, PLANES)
     def _(p):
@@ -606,7 +650,7 @@
 
         @pl.when(even_slab)
         def _():
-            psi_row(p).wait_send()
+            field_row(p).wait_send()
 
         @pl.when(is_middle)
         def _():
@@ -643,28 +687,30 @@
             pltpu.VMEM((PLANES, ROWS, NZ), f32),
             pltpu.VMEM((PLANES, ROWS, NZ), jnp.int32),
             pltpu.VMEM((GROUP, PAIRS, 2, ROWS, NZ), f32),
-            pltpu.VMEM((GROUP, OWN, 2, ROWS, NZ), f32),
             pltpu.VMEM((PLANES, GROUP, PAIRS, 2, ROWS, NZ), f32),
             pltpu.VMEM((PLANES + 1, GROUP, PAIRS, 2, ROWS, NZ), f32),
             pltpu.VMEM((GROUP, PAIRS, ROWS, NZ), f32),
             pltpu.VMEM((GROUP, PAIRS, ROWS, NZ), f32),
             pltpu.VMEM((PLANES + 1, GROUP, PAIRS, ROWS, NZ), f32),
-            pltpu.VMEM((PLANES + 1, GROUP, OWN, 2, ROWS, NZ), f32),
-            pltpu.VMEM((PLANES + 1, GROUP, OWN, 2, ROWS, NZ), f32),
+            pltpu.VMEM((PLANES, GROUP, OWN, 2, ROWS, NZ), f32),
+            pltpu.VMEM((PLANES, GROUP, OWN, 2, ROWS, NZ), f32),
+            pltpu.VMEM((GROUP, OWN, ROWS, NZ), f32),
+            pltpu.VMEM((GROUP, OWN, ROWS, NZ), f32),
             pltpu.VMEM((6, GROUP, OWN, ROWS, NZ), f32),
             pltpu.VMEM((FOLDS, 4, 6, ROWS, NZ), f32),
             pltpu.VMEM((FOLDS, 4, 3, ROWS, NZ), f32),
-            pltpu.VMEM((PLANES + 1, NCOEF, ROWS, NZ), f32),
+            pltpu.VMEM((PLANES + 1, 3, NCOEF, ROWS, NZ), f32),
             pltpu.VMEM((PLANES + 1, NCOEF, ROWS, NZ), f32),
             pltpu.VMEM((PLANES + 1, OWN, ROWS, NZ), f32),
+            pltpu.VMEM((OWN, NY, NZ), f32),
             pltpu.VMEM((PLANES, ROWS, NZ), f32),
             dma((2, PLANES)), dma, dma((2,)), dma((2,)), dma, dma, dma, dma,
             dma((PLANES + 2, GROUP - 1)), dma((PLANES + 2, GROUP - 1)),
             dma((PLANES + 1, GROUP - 1)), dma((PLANES + 1, GROUP - 1)),
             dma((PLANES + 1,)), dma((PLANES + 1, GROUP)),
             dma((PLANES + 1,)), dma((PLANES + 1,)),
-            dma((PLANES,)), dma((PLANES,)),
-            dma((PLANES, GROUP - 1)), dma((PLANES,)),
+            dma((PLANES + 1,)), dma((PLANES + 1,)),
+            dma((PLANES + 1, GROUP - 1)), dma((PLANES + 1,)),
             dma, dma, pltpu.SemaphoreType.REGULAR,
         ],
         compiler_params=pltpu.CompilerParams(

time: 55.9 us -> 55 us (0.984)
  Pallas kernels: 55.1 us -> 54.3 us
    pallas_call x1, Pallas kernels: 53.8 us -> 53 us  [local(): pl.pallas_call(kernel, out_shape=(pltpu.VMEM(residual, f32), pltpu.VMEM(g...]
where the time goes in v5:
time: 55 us; the launch traced here: 54.9 us
  Pallas kernels  54.3 us (99%)
  between operations  0.64 us (1%)
    pallas_call x1, Pallas kernels, local(): pl.pallas_call(kernel, out_shape=(pltpu.VMEM(residual, f32), pltpu.VMEM(g...  53 us
    pallas_call x1, Pallas kernels, local(): pl.pallas_call(write_out, out_shape=(jax.ShapeDtypeStruct(residual, f32),...  1.32 us

profile of v5, /device:TPU:1, one launch (start us, length us, event | category | flops | bytes accessed | tf_op | source)
XLA Modules:
  0.0 54.9 jit_solution(7356680122537488350)
XLA Ops:
  0.6 53.0 %shard_map.68 = (f32[5,3,8,32,128]{4,3,2,1,0:T(8,128)S(1)}, f32[8,8,128]{2,1,0:T(8,128)S(1)}) custom-call(f32[5,3,8,32,128]{4,3,2,1,0:T(8,128)} %state_hbm.1, f32[5,3,8,32,128]{4,3,2,1,0:T(8,128)} %adjoint_hbm.1, f32[5,3,8,32,128]{4,3,2,1,0:T(8,128)} %objective_hbm.1, f32[8,32,128]{2,1,0:T(8,128)} %density_hbm.1, s32[8,32,128]{2,1,0:T(8,128)} %region_hbm.1), custom_call_target="tpu_custom_call" | custom-call | tf_op jit(solution)/shard_map/pallas_call | solution.py:678
  53.6 1.3 %shard_map.69 = (f32[5,3,8,32,128]{4,3,2,1,0:T(8,128)}, f32[8,8,128]{2,1,0:T(8,128)}) custom-call(f32[5,3,8,32,128]{4,3,2,1,0:T(8,128)S(1)} %get-tuple-element.4.held, f32[8,8,128]{2,1,0:T(8,128)S(1)} %get-tuple-element.5.held_grad), custom_call_target="tpu_custom_call" | custom-call | tf_op jit(solution)/shard_map/pallas_call | solution.py:720

commit v6 on v5

--- a/solution.py
+++ b/solution.py
@@ -64,9 +64,9 @@
     out, grad_out,
     pot, phi, obj, dens, regn, upper, send, recv, phi_send, phi_recv, edge,
     bsend, brecv, zsend, zrecv, flux, wave, fold, field, field_edge, fix, below_sum, grad,
-    in_sems, obj_sem, mat_sems, own_sems, up_send, up_recv, low_send, low_recv,
-    f_send, f_recv, b_send, b_recv, e_send, e_recv, c_send, c_recv,
-    s_send, s_recv, x_send, x_recv, g_send, g_recv, ready,
+    in_sems, obj_sem, mat_sems, own_sem, up_send, up_recv, low_send, low_recv,
+    f_send, p_send, f_recv, b_send, z_send, b_recv, chip_send, chip_recv, mid_send, mid_recv,
+    g_send, g_recv, ready,
 ):
     me = lax.axis_index("sample")
     block = lax.axis_index("space")
@@ -102,7 +102,15 @@
     for peer in peers:
         pl.semaphore_signal(barrier, inc=1, device_id={"sample": peer}, device_id_type=mesh_id)
 
-    @pl.when(has_below)
+    ends, begins = lax.rem(block, RUN) == RUN - 1, lax.rem(block, RUN) == 0
+    waits_above, waits_below = has_above & ends, has_below & jnp.logical_not(begins)
+    tells_above, tells_below = has_above & jnp.logical_not(ends), has_below & begins
+
+    @pl.when(tells_above)
+    def _():
+        pl.semaphore_signal(barrier, inc=1, device_id=up_id, device_id_type=mesh_id)
+
+    @pl.when(tells_below)
     def _():
         pl.semaphore_signal(barrier, inc=1, device_id=down_id, device_id_type=mesh_id)
 
@@ -111,13 +119,16 @@
 
     def load(p):
         return [
-            pltpu.make_async_copy(ref.at[:, :, p], pot.at[i, p], in_sems.at[i, p])
+            pltpu.make_async_copy(ref.at[:, :, p], pot.at[p, i], in_sems.at[jnp.minimum(p, 1)])
             for i, ref in enumerate(arguments)
         ]
 
+    def all_of(ref, sem):
+        return pltpu.make_async_copy(ref, ref, sem)
+
     own = [
         pltpu.make_async_copy(
-            ref.at[:, pl.ds(1, 2), 0, slab_rows(slab)], recv.at[0, me, pl.ds(i * OWN, OWN)], own_sems.at[i]
+            ref.at[:, pl.ds(1, 2), 0, slab_rows(slab)], recv.at[0, me, pl.ds(i * OWN, OWN)], own_sem
         )
         for i, ref in enumerate(arguments)
     ]
@@ -143,58 +154,64 @@
             to_sample(
                 ref.at[:, pl.ds(1, 2), 0, slab_rows(turned(peer, block))],
                 recv.at[0, me, pl.ds(i * OWN, OWN)],
-                f_send.at[i * (PLANES + 1), r], f_recv.at[i * (PLANES + 1), r], peer,
+                f_send, f_recv.at[0], peer,
             )
-            for r, peer in enumerate(peers)
+            for peer in peers
             for i, ref in enumerate(arguments)
         ]
 
     def forward(p):
         return [
             to_sample(
-                send.at[p, turned(peer, block)], recv.at[p, me], f_send.at[p, r], f_recv.at[p, r], peer
+                send.at[p, turned(peer, block)], recv.at[p, me], f_send, f_recv.at[p], peer
             )
-            for r, peer in enumerate(peers)
+            for peer in peers
         ]
+
+    def forward_came(p):
+        all_of(recv.at[p, pl.ds(0, GROUP - 1)], f_recv.at[p]).wait()
 
     def forward_phi():
         return [
             to_sample(
                 phi_send.at[turned(peer, block)], phi_recv.at[me],
-                f_send.at[PLANES, r], f_recv.at[PLANES, r], peer,
+                p_send, f_recv.at[PLANES], peer,
             )
-            for r, peer in enumerate(peers)
+            for peer in peers
         ]
 
     def backward(p):
         return [
-            to_sample(bsend.at[p, peer], brecv.at[p, slab], b_send.at[p, r], b_recv.at[p, r], peer)
-            for r, peer in enumerate(peers)
+            to_sample(bsend.at[p, peer], brecv.at[p, slab], b_send, b_recv.at[p], peer)
+            for peer in peers
         ]
 
     def backward_zero():
         return [
-            to_sample(zsend.at[peer], zrecv.at[slab], b_send.at[PLANES, r], b_recv.at[PLANES, r], peer)
-            for r, peer in enumerate(peers)
+            to_sample(zsend.at[peer], zrecv.at[slab], z_send, b_recv.at[PLANES], peer)
+            for peer in peers
         ]
 
     top_row, end_row = pl.ds(0, 1), pl.ds(ROWS - 1, 1)
 
     def middle_row(p, q):
         source = send.at[p, 2, :, 1, top_row]
-        return to_sample(source, edge.at[p, q, :, top_row], e_send.at[p], e_recv.at[p, q], middle)
+        return to_sample(source, edge.at[p, q, :, top_row], mid_send, mid_recv.at[p], middle)
 
     def middle_phi(q):
         source = phi_send.at[2, :, top_row]
-        return to_sample(source, edge.at[PLANES, q, :, top_row], e_send.at[PLANES], e_recv.at[PLANES, q], middle)
+        return to_sample(source, edge.at[PLANES, q, :, top_row], mid_send, mid_recv.at[PLANES], middle)
+
+    def middle_came(p):
+        all_of(edge.at[p, pl.ds(0, GROUP - 1), :, top_row], mid_recv.at[p]).wait()
 
     def chip_row(p):
-        return to_sample(recv.at[p, :, :, 1, top_row], edge.at[p, :, :, top_row], c_send.at[p], c_recv.at[p], partner)
+        return to_sample(recv.at[p, :, :, 1, top_row], edge.at[p, :, :, top_row], chip_send, chip_recv.at[p], partner)
 
     def chip_phi():
         return to_sample(
             phi_recv.at[:, :, top_row], edge.at[PLANES, :, :, top_row],
-            c_send.at[PLANES], c_recv.at[PLANES], partner,
+            chip_send, chip_recv.at[PLANES], partner,
         )
 
     def last_rows(p, some):
@@ -204,15 +221,15 @@
 
     def field_row(p):
         return to_sample(
-            last_rows(p, pl.ds(0, NCOEF)), field_edge.at[p, :, end_row], s_send.at[p], s_recv.at[p], partner
+            last_rows(p, pl.ds(0, NCOEF)), field_edge.at[p, :, end_row], chip_send, chip_recv.at[p], partner
         )
 
     def fix_row(p):
         return [
             to_sample(
-                last_rows(p, pl.ds(peer * OWN, OWN)), fix.at[p, :, end_row], x_send.at[p, r], x_recv.at[p], peer
+                last_rows(p, pl.ds(peer * OWN, OWN)), fix.at[p, :, end_row], mid_send, mid_recv.at[p], peer
             )
-            for r, peer in enumerate(peers)
+            for peer in peers
         ]
 
     row_id = lax.broadcasted_iota(jnp.int32, (NY, NZ), 0)
@@ -244,30 +261,32 @@
     def slab_prior_lane(a):
         return jnp.where(slab_lane == 0, 0.0, pltpu.roll(a, 1, 1))
 
-    pl.semaphore_wait(barrier, GROUP - 1 + has_above.astype(jnp.int32))
+    pl.semaphore_wait(barrier, GROUP - 1 + waits_above.astype(jnp.int32) + waits_below.astype(jnp.int32))
     for copy in forward_first():
         copy.start()
 
-    @pl.when(has_above)
-    def _():
-        pl.semaphore_signal(ready, inc=1, device_id=up_id, device_id_type=mesh_id)
-
-    for copy in load(0):
-        copy.wait()
+    @pl.when(waits_above)
+    def _():
+        pl.semaphore_signal(ready.at[0], inc=1, device_id=up_id, device_id_type=mesh_id)
+
+    @pl.when(waits_below)
+    def _():
+        pl.semaphore_signal(ready.at[1], inc=1, device_id=down_id, device_id_type=mesh_id)
+
+    all_of(pot.at[0], in_sems.at[0]).wait()
     for i in range(2):
         for j in range(OWN):
-            phi[0, i, j] = pot[i, 0, j, 0]
-            send[0, 2, i * OWN + j, 1] = pot[i, 0, j, 2, pl.ds(2 * ROWS, ROWS), :]
+            phi[0, i, j] = pot[0, i, j, 0]
+            send[0, 2, i * OWN + j, 1] = pot[0, i, j, 2, pl.ds(2 * ROWS, ROWS), :]
+
+    all_of(pot.at[pl.ds(1, PLANES - 1)], in_sems.at[1]).wait()
 
     @pl.loop(1, PLANES)
     def _(p):
-        for copy in load(p):
-            copy.wait()
-
         for i in range(2):
             @pl.loop(0, OWN)
             def _(j):
-                phi[p, i, j] = phi[p - 1, i, j] + pot[i, p, j, 0]
+                phi[p, i, j] = phi[p - 1, i, j] + pot[p, i, j, 0]
 
     for i in range(2):
         for j in range(OWN):
@@ -293,8 +312,8 @@
         for i in range(2):
             for j in range(OWN):
                 under = phi[p - 1, i, j]
-                one = pot[i, p, j, 1] - (next_row(under) - under)
-                two = pot[i, p, j, 2] - (next_lane(under) - under)
+                one = pot[p, i, j, 1] - (next_row(under) - under)
+                two = pot[p, i, j, 2] - (next_lane(under) - under)
                 send[p, :, i * OWN + j, 0] = one.reshape(GROUP, ROWS, NZ)
                 send[p, :, i * OWN + j, 1] = two.reshape(GROUP, ROWS, NZ)
         for copy in forward(p):
@@ -331,24 +350,24 @@
     def _():
         field[0, pl.ds(1, 2)] = jnp.zeros((2, NCOEF, ROWS, NZ), jnp.float32)
 
-    for copy in own:
-        copy.wait()
-    for copy in forward_first():
-        copy.wait_recv()
+    all_of(recv.at[0, 0], own_sem).wait()
+    forward_came(0)
     up = pltpu.make_async_remote_copy(
         src_ref=recv.at[0], dst_ref=upper,
         send_sem=up_send, recv_sem=up_recv, device_id=down_id, device_id_type=mesh_id,
     )
 
+    @pl.when(tells_below)
+    def _():
+        pl.semaphore_wait(ready.at[0], 1)
+
     @pl.when(has_below)
     def _():
-        pl.semaphore_wait(ready, 1)
         up.start()
 
     for copy in material:
         copy.wait()
-    for copy in forward_phi():
-        copy.wait_recv()
+    all_of(phi_recv.at[pl.ds(0, GROUP - 1)], f_recv.at[PLANES]).wait()
 
     @pl.when(odd_slab)
     def _():
@@ -357,9 +376,8 @@
 
     @pl.when(is_middle)
     def _():
-        for peer in peers:
-            middle_phi(peer).wait_recv()
-            middle_row(0, peer).wait_recv()
+        middle_came(PLANES)
+        middle_came(0)
 
     @pl.when(even_slab)
     def _():
@@ -510,8 +528,7 @@
 
         @pl.when(p > 0)
         def _():
-            for copy in forward(p):
-                copy.wait_recv()
+            forward_came(p)
 
             @pl.when(odd_slab)
             def _():
@@ -519,8 +536,7 @@
 
             @pl.when(is_middle)
             def _():
-                for peer in peers:
-                    middle_row(p, peer).wait_recv()
+                middle_came(p)
 
             @pl.when(even_slab)
             def _():
@@ -537,6 +553,10 @@
             @pl.when(even_slab)
             def _():
                 field_row(PLANES).start()
+
+            @pl.when(tells_above)
+            def _():
+                pl.semaphore_wait(ready.at[1], 1)
 
             @pl.when(has_above)
             def _():
@@ -570,8 +590,7 @@
         return jnp.concatenate(parts, axis=0)
 
     objective.wait()
-    for copy in backward_zero():
-        copy.wait_recv()
+    all_of(zrecv.at[pl.ds(0, GROUP - 1)], b_recv.at[PLANES]).wait()
 
     @pl.when(off_middle)
     def _():
@@ -583,8 +602,7 @@
     @pl.loop(0, PLANES)
     def _(k):
         p = PLANES - 1 - k
-        for copy in backward(p):
-            copy.wait_recv()
+        all_of(brecv.at[p, pl.ds(0, GROUP - 1)], b_recv.at[p]).wait()
 
         @pl.when(off_middle)
         def _():
@@ -610,52 +628,26 @@
     def _():
         down.wait_send()
 
-    for copy in forward_first() + forward_phi() + backward_zero():
-        copy.wait_send()
+    all_of(send.at[:, pl.ds(0, GROUP - 1)], f_send).wait()
+    all_of(phi_send.at[pl.ds(0, GROUP - 1)], p_send).wait()
+    all_of(bsend.at[:, pl.ds(0, GROUP - 1)], b_send).wait()
+    all_of(zsend.at[pl.ds(0, GROUP - 1)], z_send).wait()
 
     @pl.when(off_middle)
     def _():
-        middle_phi(me).wait_send()
+        all_of(edge.at[:, 0, :, top_row], mid_send).wait()
+
+    @pl.when(is_middle)
+    def _():
+        all_of(field_edge.at[:, pl.ds(0, OWN * (GROUP - 1)), end_row], mid_send).wait()
 
     @pl.when(odd_slab)
     def _():
-        chip_phi().wait_send()
+        all_of(edge.at[:, :, :, top_row], chip_send).wait()
 
     @pl.when(even_slab)
     def _():
-        field_row(PLANES).wait_send()
-
-    @pl.when(is_middle)
-    def _():
-        for copy in fix_row(PLANES):
-            copy.wait_send()
-
-    @pl.loop(0, PLANES)
-    def _(p):
-        for copy in backward(p):
-            copy.wait_send()
-
-        @pl.when(p > 0)
-        def _():
-            for copy in forward(p):
-                copy.wait_send()
-
-        @pl.when(off_middle)
-        def _():
-            middle_row(p, me).wait_send()
-
-        @pl.when(odd_slab)
-        def _():
-            chip_row(p).wait_send()
-
-        @pl.when(even_slab)
-        def _():
-            field_row(p).wait_send()
-
-        @pl.when(is_middle)
-        def _():
-            for copy in fix_row(p):
-                copy.wait_send()
+        all_of(field_edge.at[:, :, end_row], chip_send).wait()
 
 
 def write_out(held, held_grad, out_hbm, grad_hbm, sems):
@@ -681,7 +673,7 @@
         in_specs=[hbm] * 5,
         out_specs=(vmem, vmem),
         scratch_shapes=[
-            pltpu.VMEM((2, PLANES, OWN, 3, NY, NZ), f32),
+            pltpu.VMEM((PLANES, 2, OWN, 3, NY, NZ), f32),
             pltpu.VMEM((PLANES, 2, OWN, NY, NZ), f32),
             pltpu.VMEM((OWN, 3, PLANES, NY, NZ), f32),
             pltpu.VMEM((PLANES, ROWS, NZ), f32),
@@ -704,14 +696,10 @@
             pltpu.VMEM((PLANES + 1, OWN, ROWS, NZ), f32),
             pltpu.VMEM((OWN, NY, NZ), f32),
             pltpu.VMEM((PLANES, ROWS, NZ), f32),
-            dma((2, PLANES)), dma, dma((2,)), dma((2,)), dma, dma, dma, dma,
-            dma((PLANES + 2, GROUP - 1)), dma((PLANES + 2, GROUP - 1)),
-            dma((PLANES + 1, GROUP - 1)), dma((PLANES + 1, GROUP - 1)),
-            dma((PLANES + 1,)), dma((PLANES + 1, GROUP)),
-            dma((PLANES + 1,)), dma((PLANES + 1,)),
-            dma((PLANES + 1,)), dma((PLANES + 1,)),
-            dma((PLANES + 1, GROUP - 1)), dma((PLANES + 1,)),
-            dma, dma, pltpu.SemaphoreType.REGULAR,
+            dma((2,)), dma, dma((2,)), dma, dma, dma, dma, dma,
+            dma, dma, dma((PLANES + 1,)), dma, dma, dma((PLANES + 1,)),
+            dma, dma((PLANES + 1,)), dma, dma((PLANES + 1,)),
+            dma, dma, pltpu.SemaphoreType.REGULAR((2,)),
         ],
         compiler_params=pltpu.CompilerParams(
             collective_id=0, has_side_effects=True, vmem_limit_bytes=60 * 1024 * 1024

time: 55 us -> 52.5 us (0.955)
  Pallas kernels: 54.3 us -> 51.8 us
    pallas_call x1, Pallas kernels: 53 us -> 50.4 us  [local(): pl.pallas_call(kernel, out_shape=(pltpu.VMEM(residual, f32), pltpu.VMEM(g...]
where the time goes in v6:
time: 52.5 us; the launch traced here: 52.4 us
  Pallas kernels  51.8 us (99%)
  between operations  0.64 us (1%)
    pallas_call x1, Pallas kernels, local(): pl.pallas_call(kernel, out_shape=(pltpu.VMEM(residual, f32), pltpu.VMEM(g...  50.4 us
    pallas_call x1, Pallas kernels, local(): pl.pallas_call(write_out, out_shape=(jax.ShapeDtypeStruct(residual, f32),...  1.32 us

profile of v6, /device:TPU:1, one launch (start us, length us, event | category | flops | bytes accessed | tf_op | source)
XLA Modules:
  0.0 52.4 jit_solution(2296617226584577279)
XLA Ops:
  0.6 50.4 %shard_map.68 = (f32[5,3,8,32,128]{4,3,2,1,0:T(8,128)S(1)}, f32[8,8,128]{2,1,0:T(8,128)S(1)}) custom-call(f32[5,3,8,32,128]{4,3,2,1,0:T(8,128)} %state_hbm.1, f32[5,3,8,32,128]{4,3,2,1,0:T(8,128)} %adjoint_hbm.1, f32[5,3,8,32,128]{4,3,2,1,0:T(8,128)} %objective_hbm.1, f32[8,32,128]{2,1,0:T(8,128)} %density_hbm.1, s32[8,32,128]{2,1,0:T(8,128)} %region_hbm.1), custom_call_target="tpu_custom_call" | custom-call | tf_op jit(solution)/shard_map/pallas_call | solution.py:670
  51.1 1.3 %shard_map.69 = (f32[5,3,8,32,128]{4,3,2,1,0:T(8,128)}, f32[8,8,128]{2,1,0:T(8,128)}) custom-call(f32[5,3,8,32,128]{4,3,2,1,0:T(8,128)S(1)} %get-tuple-element.4.held, f32[8,8,128]{2,1,0:T(8,128)S(1)} %get-tuple-element.5.held_grad), custom_call_target="tpu_custom_call" | custom-call | tf_op jit(solution)/shard_map/pallas_call | solution.py:708

commit v7 on v6

--- a/solution.py
+++ b/solution.py
@@ -119,12 +119,15 @@
 
     def load(p):
         return [
-            pltpu.make_async_copy(ref.at[:, :, p], pot.at[p, i], in_sems.at[jnp.minimum(p, 1)])
+            pltpu.make_async_copy(ref.at[:, :, p], pot.at[p, i], in_sems.at[min(p, 1) if isinstance(p, int) else 1])
             for i, ref in enumerate(arguments)
         ]
 
     def all_of(ref, sem):
         return pltpu.make_async_copy(ref, ref, sem)
+
+    for copy in load(0):
+        copy.start()
 
     own = [
         pltpu.make_async_copy(
@@ -135,7 +138,7 @@
     for copy in own:
         copy.start()
 
-    @pl.loop(0, PLANES)
+    @pl.loop(1, PLANES)
     def _(p):
         for copy in load(p):
             copy.start()
@@ -152,12 +155,12 @@
     def forward_first():
         return [
             to_sample(
-                ref.at[:, pl.ds(1, 2), 0, slab_rows(turned(peer, block))],
+                pot.at[0, i, :, pl.ds(1, 2), slab_rows(turned(peer, block))],
                 recv.at[0, me, pl.ds(i * OWN, OWN)],
                 f_send, f_recv.at[0], peer,
             )
             for peer in peers
-            for i, ref in enumerate(arguments)
+            for i in range(2)
         ]
 
     def forward(p):
@@ -262,6 +265,7 @@
         return jnp.where(slab_lane == 0, 0.0, pltpu.roll(a, 1, 1))
 
     pl.semaphore_wait(barrier, GROUP - 1 + waits_above.astype(jnp.int32) + waits_below.astype(jnp.int32))
+    all_of(pot.at[0], in_sems.at[0]).wait()
     for copy in forward_first():
         copy.start()
 
@@ -273,7 +277,6 @@
     def _():
         pl.semaphore_signal(ready.at[1], inc=1, device_id=down_id, device_id_type=mesh_id)
 
-    all_of(pot.at[0], in_sems.at[0]).wait()
     for i in range(2):
         for j in range(OWN):
             phi[0, i, j] = pot[0, i, j, 0]

time: 52.5 us -> 52.7 us (level)
  no operation moved by 1% of the time
where the time goes in v7:
time: 52.7 us; the launch traced here: 52.6 us
  Pallas kernels  52 us (99%)
  between operations  0.64 us (1%)
    pallas_call x1, Pallas kernels, local(): pl.pallas_call(kernel, out_shape=(pltpu.VMEM(residual, f32), pltpu.VMEM(g...  50.6 us
    pallas_call x1, Pallas kernels, local(): pl.pallas_call(write_out, out_shape=(jax.ShapeDtypeStruct(residual, f32),...  1.32 us

profile of v7, /device:TPU:1, one launch (start us, length us, event | category | flops | bytes accessed | tf_op | source)
XLA Modules:
  0.0 52.6 jit_solution(16508621522250519418)
XLA Ops:
  0.6 50.6 %shard_map.68 = (f32[5,3,8,32,128]{4,3,2,1,0:T(8,128)S(1)}, f32[8,8,128]{2,1,0:T(8,128)S(1)}) custom-call(f32[5,3,8,32,128]{4,3,2,1,0:T(8,128)} %state_hbm.1, f32[5,3,8,32,128]{4,3,2,1,0:T(8,128)} %adjoint_hbm.1, f32[5,3,8,32,128]{4,3,2,1,0:T(8,128)} %objective_hbm.1, f32[8,32,128]{2,1,0:T(8,128)} %density_hbm.1, s32[8,32,128]{2,1,0:T(8,128)} %region_hbm.1), custom_call_target="tpu_custom_call" | custom-call | tf_op jit(solution)/shard_map/pallas_call | solution.py:673
  51.3 1.3 %shard_map.69 = (f32[5,3,8,32,128]{4,3,2,1,0:T(8,128)}, f32[8,8,128]{2,1,0:T(8,128)}) custom-call(f32[5,3,8,32,128]{4,3,2,1,0:T(8,128)S(1)} %get-tuple-element.4.held, f32[8,8,128]{2,1,0:T(8,128)S(1)} %get-tuple-element.5.held_grad), custom_call_target="tpu_custom_call" | custom-call | tf_op jit(solution)/shard_map/pallas_call | solution.py:711

commit v8 on v7

--- a/solution.py
+++ b/solution.py
@@ -18,6 +18,7 @@
 FOLDS = NT // 4 + 1
 PAIRS = 2 * OWN
 RUN = 4
+HALF = PLANES // 2
 
 magnet_reluct = 0.95
 iron_floor = 0.05
@@ -166,47 +167,49 @@
     def forward(p):
         return [
             to_sample(
-                send.at[p, turned(peer, block)], recv.at[p, me], f_send, f_recv.at[p], peer
+                send.at[p, turned(peer, block)], recv.at[p, me], f_send, f_recv.at[3 - p // HALF], peer
             )
             for peer in peers
         ]
 
-    def forward_came(p):
-        all_of(recv.at[p, pl.ds(0, GROUP - 1)], f_recv.at[p]).wait()
+    groups = (pl.ds(0, 1), pl.ds(PLANES, 1), pl.ds(HALF, HALF), pl.ds(1, HALF - 1))
+
+    def forward_came(g):
+        all_of(recv.at[groups[g], pl.ds(0, GROUP - 1)], f_recv.at[g]).wait()
 
     def forward_phi():
         return [
             to_sample(
                 phi_send.at[turned(peer, block)], phi_recv.at[me],
-                p_send, f_recv.at[PLANES], peer,
+                p_send, f_recv.at[1], peer,
             )
             for peer in peers
         ]
 
-    def backward(p):
+    def backward(p, g):
         return [
-            to_sample(bsend.at[p, peer], brecv.at[p, slab], b_send, b_recv.at[p], peer)
+            to_sample(bsend.at[p, peer], brecv.at[p, slab], b_send, b_recv.at[g], peer)
             for peer in peers
         ]
 
     def backward_zero():
         return [
-            to_sample(zsend.at[peer], zrecv.at[slab], z_send, b_recv.at[PLANES], peer)
+            to_sample(zsend.at[peer], zrecv.at[slab], z_send, b_recv.at[2], peer)
             for peer in peers
         ]
 
     top_row, end_row = pl.ds(0, 1), pl.ds(ROWS - 1, 1)
 
-    def middle_row(p, q):
+    def middle_row(p, q, g):
         source = send.at[p, 2, :, 1, top_row]
-        return to_sample(source, edge.at[p, q, :, top_row], mid_send, mid_recv.at[p], middle)
+        return to_sample(source, edge.at[p, q, :, top_row], mid_send, mid_recv.at[g], middle)
 
     def middle_phi(q):
         source = phi_send.at[2, :, top_row]
-        return to_sample(source, edge.at[PLANES, q, :, top_row], mid_send, mid_recv.at[PLANES], middle)
-
-    def middle_came(p):
-        all_of(edge.at[p, pl.ds(0, GROUP - 1), :, top_row], mid_recv.at[p]).wait()
+        return to_sample(source, edge.at[PLANES, q, :, top_row], mid_send, mid_recv.at[1], middle)
+
+    def middle_came(g):
+        all_of(edge.at[groups[g], pl.ds(0, GROUP - 1), :, top_row], mid_recv.at[g]).wait()
 
     def chip_row(p):
         return to_sample(recv.at[p, :, :, 1, top_row], edge.at[p, :, :, top_row], chip_send, chip_recv.at[p], partner)
@@ -227,10 +230,10 @@
             last_rows(p, pl.ds(0, NCOEF)), field_edge.at[p, :, end_row], chip_send, chip_recv.at[p], partner
         )
 
-    def fix_row(p):
+    def fix_row(p, g):
         return [
             to_sample(
-                last_rows(p, pl.ds(peer * OWN, OWN)), fix.at[p, :, end_row], mid_send, mid_recv.at[p], peer
+                last_rows(p, pl.ds(peer * OWN, OWN)), fix.at[p, :, end_row], mid_send, mid_recv.at[g], peer
             )
             for peer in peers
         ]
@@ -301,7 +304,7 @@
     @pl.when(off_middle)
     def _():
         middle_phi(me).start()
-        middle_row(0, me).start()
+        middle_row(0, me, 0).start()
 
     @pl.when(is_middle)
     def _():
@@ -324,7 +327,7 @@
 
         @pl.when(off_middle)
         def _():
-            middle_row(p, me).start()
+            middle_row(p, me, 3 - p // HALF).start()
 
         @pl.when(is_middle)
         def _():
@@ -370,7 +373,7 @@
 
     for copy in material:
         copy.wait()
-    all_of(phi_recv.at[pl.ds(0, GROUP - 1)], f_recv.at[PLANES]).wait()
+    all_of(phi_recv.at[pl.ds(0, GROUP - 1)], f_recv.at[1]).wait()
 
     @pl.when(odd_slab)
     def _():
@@ -379,7 +382,7 @@
 
     @pl.when(is_middle)
     def _():
-        middle_came(PLANES)
+        middle_came(1)
         middle_came(0)
 
     @pl.when(even_slab)
@@ -476,14 +479,14 @@
                     ]
                     field[p + 1, c, coef_index(kind, m)] = combine(terms, scales)
 
-    def give_back(p):
+    def give_back(p, g):
         @pl.when(odd_slab)
         def _():
             field_row(p).wait_recv()
 
         @pl.when(is_middle)
         def _():
-            for copy in fix_row(p):
+            for copy in fix_row(p, g):
                 copy.start()
 
             fix[p] = field[p + 1, 0, pl.ds(me * OWN, OWN)]
@@ -497,7 +500,7 @@
                 bsend[p, q, j, 0] = (field[p, 2, at] - two) - (slab_prior_lane(zero) - zero)
                 bsend[p, q, j, 1] = (slab_prior_row(zero, row) - zero) - (field[p, 1, at] - one)
 
-        for copy in backward(p):
+        for copy in backward(p, g):
             copy.start()
         brecv[p, slab] = bsend[p, me]
 
@@ -508,7 +511,7 @@
 
         @pl.when(is_middle)
         def _():
-            for copy in fix_row(PLANES):
+            for copy in fix_row(PLANES, 1):
                 copy.start()
 
             fix[PLANES] = field[PLANES, 2, pl.ds(me * OWN, OWN)]
@@ -521,26 +524,32 @@
                 row = field_edge[PLANES, at, end_row, :]
                 zsend[q, j] = (slab_prior_lane(one) - one) - (slab_prior_row(two, row) - two)
 
-        for copy in backward_zero():
-            copy.start()
+        @pl.when(has_below)
+        def _():
+            for copy in backward_zero():
+                copy.start()
+
         zrecv[slab] = zsend[me]
 
     @pl.loop(0, PLANES)
     def _(k):
         p = PLANES - 1 - k
 
+        for g, at in ((2, PLANES - 1), (3, HALF - 1)):
+            @pl.when(p == at)
+            def _():
+                forward_came(g)
+
+                @pl.when(is_middle)
+                def _():
+                    middle_came(g)
+
         @pl.when(p > 0)
         def _():
-            forward_came(p)
-
             @pl.when(odd_slab)
             def _():
                 chip_row(p).start()
 
-            @pl.when(is_middle)
-            def _():
-                middle_came(p)
-
             @pl.when(even_slab)
             def _():
                 chip_row(p).wait_recv()
@@ -569,13 +578,13 @@
 
         @pl.when(k > 0)
         def _():
-            give_back(p + 1)
+            give_back(p + 1, 1)
 
     @pl.when(has_below)
     def _():
         down.wait_recv()
 
-    give_back(0)
+    give_back(0, 0)
 
     swap = to_sample(grad, grad_out, g_send, g_recv, lax.rem(me + 2, GROUP))
 
@@ -593,23 +602,33 @@
         return jnp.concatenate(parts, axis=0)
 
     objective.wait()
-    all_of(zrecv.at[pl.ds(0, GROUP - 1)], b_recv.at[PLANES]).wait()
+    all_of(brecv.at[pl.ds(1, PLANES - 1), pl.ds(0, GROUP - 1)], b_recv.at[1]).wait()
 
     @pl.when(off_middle)
     def _():
-        fix_row(PLANES)[0].wait_recv()
-
-    for j in range(OWN):
-        below_sum[j] = fixed([zrecv[q, j] for q in range(GROUP)], PLANES, j, -1)
+        all_of(fix.at[pl.ds(1, PLANES), :, end_row], mid_recv.at[1]).wait()
+
+    @pl.when(has_below)
+    def _():
+        all_of(zrecv.at[pl.ds(0, GROUP - 1)], b_recv.at[2]).wait()
+        for j in range(OWN):
+            below_sum[j] = fixed([zrecv[q, j] for q in range(GROUP)], PLANES, j, -1)
+
+    @pl.when(jnp.logical_not(has_below))
+    def _():
+        below_sum[...] = jnp.zeros_like(below_sum)
 
     @pl.loop(0, PLANES)
     def _(k):
         p = PLANES - 1 - k
-        all_of(brecv.at[p, pl.ds(0, GROUP - 1)], b_recv.at[p]).wait()
-
-        @pl.when(off_middle)
-        def _():
-            fix_row(p)[0].wait_recv()
+
+        @pl.when(p == 0)
+        def _():
+            all_of(brecv.at[0, pl.ds(0, GROUP - 1)], b_recv.at[0]).wait()
+
+            @pl.when(off_middle)
+            def _():
+                all_of(fix.at[0, :, end_row], mid_recv.at[0]).wait()
 
         for j in range(OWN):
             zero = below_sum[j]
@@ -619,6 +638,13 @@
                 out[j, c, p] = obj[j, c, p] - part
             below_sum[j] = zero - (prior_row(one) - one) - (prior_lane(two) - two)
 
+    @pl.when(jnp.logical_not(has_below))
+    def _():
+        @pl.loop(0, PLANES)
+        def _(p):
+            for j in range(OWN):
+                out[j, 0, p] = out[j, 0, p] + below_sum[j]
+
     @pl.when(swaps)
     def _():
         swap.wait()
@@ -634,7 +660,10 @@
     all_of(send.at[:, pl.ds(0, GROUP - 1)], f_send).wait()
     all_of(phi_send.at[pl.ds(0, GROUP - 1)], p_send).wait()
     all_of(bsend.at[:, pl.ds(0, GROUP - 1)], b_send).wait()
-    all_of(zsend.at[pl.ds(0, GROUP - 1)], z_send).wait()
+
+    @pl.when(has_below)
+    def _():
+        all_of(zsend.at[pl.ds(0, GROUP - 1)], z_send).wait()
 
     @pl.when(off_middle)
     def _():
@@ -700,8 +729,8 @@
             pltpu.VMEM((OWN, NY, NZ), f32),
             pltpu.VMEM((PLANES, ROWS, NZ), f32),
             dma((2,)), dma, dma((2,)), dma, dma, dma, dma, dma,
-            dma, dma, dma((PLANES + 1,)), dma, dma, dma((PLANES + 1,)),
-            dma, dma((PLANES + 1,)), dma, dma((PLANES + 1,)),
+            dma, dma, dma((4,)), dma, dma, dma((3,)),
+            dma, dma((PLANES + 1,)), dma, dma((4,)),
             dma, dma, pltpu.SemaphoreType.REGULAR((2,)),
         ],
         compiler_params=pltpu.CompilerParams(

time: 52.7 us -> 52 us (0.987)
  Pallas kernels: 52 us -> 51.1 us
    pallas_call x1, Pallas kernels: 50.6 us -> 49.7 us  [local(): pl.pallas_call(kernel, out_shape=(pltpu.VMEM(residual, f32), pltpu.VMEM(g...]
where the time goes in v8:
time: 52 us; the launch traced here: 51.7 us
  Pallas kernels  51.1 us (98%)
  between operations  0.64 us (1%)
    pallas_call x1, Pallas kernels, local(): pl.pallas_call(kernel, out_shape=(pltpu.VMEM(residual, f32), pltpu.VMEM(g...  49.7 us
    pallas_call x1, Pallas kernels, local(): pl.pallas_call(write_out, out_shape=(jax.ShapeDtypeStruct(residual, f32),...  1.32 us

profile of v8, /device:TPU:1, one launch (start us, length us, event | category | flops | bytes accessed | tf_op | source)
XLA Modules:
  0.0 51.7 jit_solution(16068175891099037955)
XLA Ops:
  0.6 49.7 %shard_map.68 = (f32[5,3,8,32,128]{4,3,2,1,0:T(8,128)S(1)}, f32[8,8,128]{2,1,0:T(8,128)S(1)}) custom-call(f32[5,3,8,32,128]{4,3,2,1,0:T(8,128)} %state_hbm.1, f32[5,3,8,32,128]{4,3,2,1,0:T(8,128)} %adjoint_hbm.1, f32[5,3,8,32,128]{4,3,2,1,0:T(8,128)} %objective_hbm.1, f32[8,32,128]{2,1,0:T(8,128)} %density_hbm.1, s32[8,32,128]{2,1,0:T(8,128)} %region_hbm.1), custom_call_target="tpu_custom_call" | custom-call | tf_op jit(solution)/shard_map/pallas_call | solution.py:702
  50.4 1.3 %shard_map.69 = (f32[5,3,8,32,128]{4,3,2,1,0:T(8,128)}, f32[8,8,128]{2,1,0:T(8,128)}) custom-call(f32[5,3,8,32,128]{4,3,2,1,0:T(8,128)S(1)} %get-tuple-element.4.held, f32[8,8,128]{2,1,0:T(8,128)S(1)} %get-tuple-element.5.held_grad), custom_call_target="tpu_custom_call" | custom-call | tf_op jit(solution)/shard_map/pallas_call | solution.py:740

commit v9 on v8

--- a/solution.py
+++ b/solution.py
@@ -65,7 +65,7 @@
     out, grad_out,
     pot, phi, obj, dens, regn, upper, send, recv, phi_send, phi_recv, edge,
     bsend, brecv, zsend, zrecv, flux, wave, fold, field, field_edge, fix, below_sum, grad,
-    in_sems, obj_sem, mat_sems, own_sem, up_send, up_recv, low_send, low_recv,
+    in_sems, obj_sem, mat_sems, up_send, up_recv, low_send, low_recv,
     f_send, p_send, f_recv, b_send, z_send, b_recv, chip_send, chip_recv, mid_send, mid_recv,
     g_send, g_recv, ready,
 ):
@@ -130,15 +130,6 @@
     for copy in load(0):
         copy.start()
 
-    own = [
-        pltpu.make_async_copy(
-            ref.at[:, pl.ds(1, 2), 0, slab_rows(slab)], recv.at[0, me, pl.ds(i * OWN, OWN)], own_sem
-        )
-        for i, ref in enumerate(arguments)
-    ]
-    for copy in own:
-        copy.start()
-
     @pl.loop(1, PLANES)
     def _(p):
         for copy in load(p):
@@ -283,6 +274,7 @@
     for i in range(2):
         for j in range(OWN):
             phi[0, i, j] = pot[0, i, j, 0]
+            recv[0, me, i * OWN + j] = pot[0, i, j, pl.ds(1, 2), slab_rows(slab), :]
             send[0, 2, i * OWN + j, 1] = pot[0, i, j, 2, pl.ds(2 * ROWS, ROWS), :]
 
     all_of(pot.at[pl.ds(1, PLANES - 1)], in_sems.at[1]).wait()
@@ -356,7 +348,6 @@
     def _():
         field[0, pl.ds(1, 2)] = jnp.zeros((2, NCOEF, ROWS, NZ), jnp.float32)
 
-    all_of(recv.at[0, 0], own_sem).wait()
     forward_came(0)
     up = pltpu.make_async_remote_copy(
         src_ref=recv.at[0], dst_ref=upper,
@@ -728,7 +719,7 @@
             pltpu.VMEM((PLANES + 1, OWN, ROWS, NZ), f32),
             pltpu.VMEM((OWN, NY, NZ), f32),
             pltpu.VMEM((PLANES, ROWS, NZ), f32),
-            dma((2,)), dma, dma((2,)), dma, dma, dma, dma, dma,
+            dma((2,)), dma, dma((2,)), dma, dma, dma, dma,
             dma, dma, dma((4,)), dma, dma, dma((3,)),
             dma, dma((PLANES + 1,)), dma, dma((4,)),
             dma, dma, pltpu.SemaphoreType.REGULAR((2,)),

time: 52 us -> 52 us (level)
  no operation moved by 1% of the time
where the time goes in v9:
time: 52 us; the launch traced here: 51.7 us
  Pallas kernels  51.1 us (98%)
  between operations  0.64 us (1%)
    pallas_call x1, Pallas kernels, local(): pl.pallas_call(kernel, out_shape=(pltpu.VMEM(residual, f32), pltpu.VMEM(g...  49.7 us
    pallas_call x1, Pallas kernels, local(): pl.pallas_call(write_out, out_shape=(jax.ShapeDtypeStruct(residual, f32),...  1.32 us

profile of v9, /device:TPU:1, one launch (start us, length us, event | category | flops | bytes accessed | tf_op | source)
XLA Modules:
  0.0 51.7 jit_solution(12230311762920165444)
XLA Ops:
  0.6 49.7 %shard_map.68 = (f32[5,3,8,32,128]{4,3,2,1,0:T(8,128)S(1)}, f32[8,8,128]{2,1,0:T(8,128)S(1)}) custom-call(f32[5,3,8,32,128]{4,3,2,1,0:T(8,128)} %state_hbm.1, f32[5,3,8,32,128]{4,3,2,1,0:T(8,128)} %adjoint_hbm.1, f32[5,3,8,32,128]{4,3,2,1,0:T(8,128)} %objective_hbm.1, f32[8,32,128]{2,1,0:T(8,128)} %density_hbm.1, s32[8,32,128]{2,1,0:T(8,128)} %region_hbm.1), custom_call_target="tpu_custom_call" | custom-call | tf_op jit(solution)/shard_map/pallas_call | solution.py:693
  50.4 1.3 %shard_map.69 = (f32[5,3,8,32,128]{4,3,2,1,0:T(8,128)}, f32[8,8,128]{2,1,0:T(8,128)}) custom-call(f32[5,3,8,32,128]{4,3,2,1,0:T(8,128)S(1)} %get-tuple-element.4.held, f32[8,8,128]{2,1,0:T(8,128)S(1)} %get-tuple-element.5.held_grad), custom_call_target="tpu_custom_call" | custom-call | tf_op jit(solution)/shard_map/pallas_call | solution.py:731
